TPU v7x, 512 devices: a whole 4x8x8 slice. The times are simulated.
512 devices in a mesh: lat: 64 (over z_lo, y, core), rad: 8 (over x, z_hi).
Axes of the slice: x: 4, y: 8, z: 8 (z_hi: 2, z_lo: 4; z = z_hi * 4 + z_lo), core: 2. Of those that a mesh axis runs over, the one named last changes fastest.
Arguments:
- displacement: float32 [1024, 32, 2048], P('lat', 'rad'), may hold values from -3 to 3
- memory: float32 [1024, 32, 2048], P('lat', 'rad'), may hold values from -3 to 3
- ice_class: int32 [1024, 2048], P('lat'), may hold values from 0 to 7
- material: int32 [1024, 32], P('lat', 'rad'), may hold values from 0 to 7
- mu_table: float32 [8], replicated, may hold values from 0.5 to 4
- decay_table: float32 [8], replicated, may hold values from 0.2 to 0.95
- contrast_table: float32 [8], replicated, may hold values from 0.5 to 2
- gravity_kernel: float32 [256, 32, 32], P('lat', 'rad'), may hold values from -1 to 1
Outputs:
- displacement_out: float32 [1024, 32, 2048], P('lat', 'rad')
- memory_out: float32 [1024, 32, 2048], P('lat', 'rad')
- potential: float32 [1024, 32, 2048], P('lat', 'rad')
All inputs are finite; a program needn't handle non-finite values.
Results may differ from a plain program's by a relative error of at most 0.0028.
Values sent between devices are 32-bit elements; how exact they have to be, the bound alone decides.
No kernel may reach another device: no remote copies, remote signals or barrier semaphores. Data moves between devices by JAX's collectives and lax.ppermute only.
A program may use at most 64 MiB of HBM per device.

v0:
```python
import functools

import jax
import jax.numpy as jnp
from jax import lax
from jax.sharding import Mesh
from jax.sharding import PartitionSpec as P

MODES = 256
LAT_RAD = ("lat_0", "lat_1", "lat_2", "rad_0", "rad_1")
LAT = ("lat_0", "lat_1", "lat_2")
RAD = ("rad_0", "rad_1")


load_scale = 0.5
kappa_shift = 0.5
relax_factor = 0.8
coupling = 2.0


def extended(x, sides, width):
    edges = {}
    for axis, dim in sides:
        devices, length = (lax.axis_size(axis), x.shape[dim])
        up = [(i, (i + 1) % devices) for i in range(devices - 1)]
        last = lax.slice_in_dim(x, length - width, length, axis=dim)
        first = lax.slice_in_dim(x, 0, width, axis=dim)
        edges[dim] = (
            lax.ppermute(last, axis, up),
            lax.ppermute(first, axis, [(b, a) for a, b in up]),
        )
    done = []
    for _, dim in sides:
        low, high = edges[dim]
        around = [(width, width) if d in done else (0, 0) for d in range(x.ndim)]
        x = jnp.concatenate([jnp.pad(low, around), x, jnp.pad(high, around)], axis=dim)
        done.append(dim)
    return x


def over_axes(x, axes):
    return functools.reduce(lax.psum, axes, x)


def copy_for_each(x, axis):
    copies = jnp.broadcast_to(x, (lax.axis_size(axis), *x.shape))
    return lax.all_to_all(copies, axis, split_axis=0, concat_axis=0, tiled=True)


def laid_out(blocks, dim):
    blocks = jnp.moveaxis(blocks, 0, dim)
    shape = blocks.shape
    return blocks.reshape(*shape[:dim], shape[dim] * shape[dim + 1], *shape[dim + 2 :])


def gathered_copies(x, axis, dim):
    blocks = copy_for_each(x, axis)
    return laid_out(blocks, dim)


def lookup(material, table):
    onehot = (
        material[:, :, None] == jnp.arange(table.shape[0], dtype=jnp.int32)[None, None, :]
    ).astype(jnp.float32)
    return jnp.sum(onehot * table[None, None, :], axis=-1)


def fourier_table(nlon, modes):
    longitude = jnp.arange(nlon, dtype=jnp.int32)
    order = jnp.arange(modes, dtype=jnp.int32)
    phase = (longitude[:, None] * order[None, :] % nlon).astype(jnp.float32)
    angle = phase * (2.0 * jnp.pi / nlon)
    scale = jnp.sqrt(jnp.float32(2.0) / nlon)
    return scale * jnp.concatenate([jnp.cos(angle), jnp.sin(angle)], axis=1)


def legendre(cosine, count):

    def step(carry, degree):
        before, current = carry
        nextone = ((2.0 * degree + 1.0) * cosine * current - degree * before) / (degree + 1.0)
        return ((current, nextone), current * jnp.sqrt(degree + 0.5))

    start = (jnp.zeros_like(cosine), jnp.ones_like(cosine))
    _, rows = lax.scan(step, start, jnp.arange(count, dtype=jnp.float32), unroll=16)
    return rows


def sweep(field, memory, source, stiff, decay):
    padded = extended(field, ((LAT, 0), (RAD, 1)), 1)
    beside = padded[2:, 1:-1] + padded[:-2, 1:-1] + padded[1:-1, 2:] + padded[1:-1, :-2]
    beside = beside + jnp.roll(field, 1, axis=2) + jnp.roll(field, -1, axis=2)
    diagonal = stiff * (6.0 + kappa_shift)
    applied = diagonal * field - stiff * beside
    update = relax_factor * (source - memory - applied) / diagonal
    return (field + update, decay * memory + stiff * update)


def per_device(
    displacement, memory, ice_class, material, mu_table, decay_table, contrast_table, gravity_kernel
):
    lat_dev, r_dev, nlon = displacement.shape
    lat_count = lax.axis_size(LAT)
    rad_count = lax.axis_size(RAD)
    lat_index = lax.axis_index(LAT)
    rad_index = lax.axis_index(RAD)
    total_lat = lat_count * lat_dev
    total_rad = rad_count * r_dev
    degrees = gravity_kernel.shape[0] * lat_count
    cols = 2 * MODES
    stiff = lookup(material, mu_table)[:, :, None]
    decay = lookup(material, decay_table)[:, :, None]
    contrast = lookup(material, contrast_table)[:, :, None]
    layer_pos = (rad_index * r_dev + jnp.arange(r_dev, dtype=jnp.int32) + 1).astype(
        jnp.float32
    ) / total_rad
    source = load_scale * ice_class.astype(jnp.float32)[:, None, :] * layer_pos[None, :, None]
    theta_all = (jnp.arange(total_lat, dtype=jnp.float32) + 0.5) * (jnp.pi / total_lat)
    basis_all = legendre(jnp.cos(theta_all), degrees)
    weighted_all = basis_all * (jnp.pi / total_lat * jnp.sin(theta_all))[None, :]
    field, mem = (displacement, memory)
    for step in range(3):
        field, mem = sweep(field, mem, source, stiff, decay)
    rho = contrast * field
    cells = total_lat * total_rad * nlon
    local_mass = jnp.sum(rho)
    table = fourier_table(nlon, MODES)
    column_sums = jnp.sum(table, axis=0)
    weight_sums = jnp.sum(weighted_all, axis=1)
    spectra = jnp.dot(
        rho.reshape(lat_dev * r_dev, nlon), table, precision=lax.Precision.HIGHEST
    ).reshape(lat_dev, r_dev * cols)
    mass = over_axes(local_mass, LAT_RAD)
    columns = cols // lat_count
    spread = lax.all_to_all(
        spectra.reshape(lat_dev, r_dev, cols), LAT, split_axis=2, concat_axis=0, tiled=True
    )
    coef_cols = jnp.dot(
        weighted_all, spread.reshape(total_lat, r_dev * columns), precision=lax.Precision.HIGHEST
    ).reshape(degrees, r_dev, columns)
    own_columns = lax.dynamic_slice_in_dim(column_sums, lat_index * columns, columns, 0)
    coef_cols = coef_cols - mass / cells * weight_sums[:, None, None] * own_columns[None, None, :]
    kernel_every = gathered_copies(gravity_kernel, LAT, 0)
    phi_cols = jnp.einsum(
        "nab,nbk->nak",
        kernel_every,
        gathered_copies(coef_cols, RAD, 1),
        precision=lax.Precision.HIGHEST,
    )
    synth_cols = jnp.dot(
        basis_all.T, phi_cols.reshape(degrees, r_dev * columns), precision=lax.Precision.HIGHEST
    ).reshape(total_lat, r_dev, columns)
    synth = lax.all_to_all(synth_cols, LAT, split_axis=0, concat_axis=2, tiled=True)
    potential = jnp.dot(
        synth.reshape(lat_dev * r_dev, cols), table.T, precision=lax.Precision.HIGHEST
    ).reshape(lat_dev, r_dev, nlon)
    loaded = source + coupling * potential
    for step in range(3):
        field, mem = sweep(field, mem, loaded, stiff, decay)
    return (field, mem, potential)


def solution(mesh):
    torus = Mesh(mesh.devices.reshape(4, 8, 2, 4, 2), ("lat_0", "lat_1", "lat_2", "rad_0", "rad_1"))
    in_specs = (
        P(LAT, RAD, None),
        P(LAT, RAD, None),
        P(LAT, None),
        P(LAT, RAD),
        P(),
        P(),
        P(),
        P(LAT, RAD, None),
    )
    out_specs = (P(LAT, RAD, None), P(LAT, RAD, None), P(LAT, RAD, None))
    return jax.shard_map(
        per_device, mesh=torus, in_specs=in_specs, out_specs=out_specs, check_vma=False
    )
```

profile of v0, /device:TPU:64, one launch (start us, length us, event | category | flops | bytes accessed | tf_op | source)
XLA Modules:
  0.0 1048.5 jit_solution(349742536556643382)
XLA Ops:
  4.0 10.6 %collective-permute-start.3 = (f32[16,1,2048]{2,0,1:T(8,128)}, f32[16,1,2048]{2,0,1:T(8,128)S(1)}, u32[]{:S(2)}, u32[]{:S(2)}) collective-permute-start(f32[16,1,2048]{2,0,1:T(8,128)} %get-tuple-element.258), channel_id=1, source_target_pairs={{0,1},{1,2},{2,3},{3,4},{4,5},{5,6},{6,7},{8,9},{9,10},{10,11},{11... | collective-permute-start | bytes 393224 | tf_op jit(solution)/shard_map/ppermute | solution.py:29
  24.9 9.2 all-to-all-start.2
  35.9 9.0 fusion.80
  45.2 735.3 %while.16 = (s32[]{:T(128)}, f32[1024]{0:T(1024)S(1)}, f32[1024]{0:T(1024)S(1)}, f32[16,16,1024]{2,1,0:T(8,128)}, f32[16,16]{1,0:T(8,128)S(1)}, /*index=5*/s32[]...) while((s32[]{:T(128)}, f32[1024]{0:T(1024)S(1)}, f32[1024]{0:T(1024)S(1)}, ...), condition=%wide.region_3.4_spmd.clone.clone, body=%wide.region_2.0_spmd.clone.clone.sunk | while | flops 143427 | bytes 423996 | solution.py:85
  69.7 9.4 broadcast_multiply_fusion.25
  115.6 9.4 broadcast_multiply_fusion.25
  161.6 9.4 broadcast_multiply_fusion.25
  207.5 9.4 broadcast_multiply_fusion.25
  253.5 9.4 broadcast_multiply_fusion.25
  299.4 9.4 broadcast_multiply_fusion.25
  345.4 9.4 broadcast_multiply_fusion.25
  391.3 9.4 broadcast_multiply_fusion.25
  437.3 9.4 broadcast_multiply_fusion.25
  483.2 9.4 broadcast_multiply_fusion.25
  529.2 9.4 broadcast_multiply_fusion.25
  575.2 9.4 broadcast_multiply_fusion.25
  621.1 9.4 broadcast_multiply_fusion.25
  667.1 9.4 broadcast_multiply_fusion.25
  713.0 9.4 broadcast_multiply_fusion.25
  759.0 9.4 broadcast_multiply_fusion.25
  792.4 9.8 collective-permute-start.7
  817.9 8.5 collective-permute-start.11
  838.9 9.7 psum.35
  853.0 14.8 %psum.36 = f32[]{:T(128)} all-reduce(f32[]{:T(128)} %psum.35), channel_id=1, replica_groups=mesh['lat_0'=4,'lat_1'=8,'lat_2'=2,'rad_0'=4,'rad_1'=2] {'lat_1'}, use_global_device_ids=true, to_apply=%region_7.8 | all-reduce | flops 1 | bytes 8 | tf_op jit(solution)/shard_map/psum | solution.py:42
  874.9 15.2 %psum.38 = f32[]{:T(128)} all-reduce(f32[]{:T(128)} %psum.37), channel_id=1, replica_groups=mesh['lat_0'=4,'lat_1'=8,'lat_2'=2,'rad_0'=4,'rad_1'=2] {'rad_0'}, use_global_device_ids=true, to_apply=%region_9.10 | all-reduce | flops 1 | bytes 8 | tf_op jit(solution)/shard_map/psum | solution.py:42
  897.4 9.4 psum.39
  924.6 11.7 %all-to-all-done.1 = f32[8,256,4,8]{1,3,2,0:T(8,128)S(1)} async-done(((f32[8,256,4,8]{1,3,2,0:T(8,128)}), f32[8,256,4,8]{1,3,2,0:T(8,128)S(1)}, u32[]{:S(2)}, u32[]{:S(2)}) %all-to-all-start.1) | async-done | bytes 262176 | tf_op jit(solution)/shard_map/all_to_all | solution.py:47
  951.1 9.0 all-to-all-start.3
  962.1 9.1 collective-permute-start.15
  985.4 15.2 %fusion.66 = f32[16,4,2048]{2,0,1:T(8,128)S(1)} fusion(f32[2048,256]{1,0:T(8,128)S(1)} %get-tuple-element.265, f32[2048,256]{1,0:T(8,128)} %get-tuple-element.266, f32[64,16,4,8]{1,3,0,2:T(8,128)} %copy.115), kind=kOutput, calls=%fused_computation.86 | convolution fusion | flops 807403520 | bytes 4849664 | tf_op jit(solution)/shard_map/dot_general | solution.py:154
  1004.1 8.5 collective-permute-start.19
  1027.3 8.5 collective-permute-start.23
  (304 shorter events, 250.5 us)
Async XLA Ops:
  2.7 781.8 %collective-permute-start.2 = (f32[16,1,2048]{2,0,1:T(8,128)}, f32[16,1,2048]{2,0,1:T(8,128)S(1)}, u32[]{:S(2)}, u32[]{:S(2)}) collective-permute-start(f32[16,1,2048]{2,0,1:T(8,128)} %get-tuple-element.257), channel_id=1, source_target_pairs={{1,0},{2,1},{3,2},{4,3},{5,4},{6,5},{7,6},{9,8},{10,9},{11,10},{12... | collective-permute-start | bytes 393224 | tf_op jit(solution)/shard_map/ppermute | solution.py:30
  4.0 780.6 %collective-permute-start.3 = (f32[16,1,2048]{2,0,1:T(8,128)}, f32[16,1,2048]{2,0,1:T(8,128)S(1)}, u32[]{:S(2)}, u32[]{:S(2)}) collective-permute-start(f32[16,1,2048]{2,0,1:T(8,128)} %get-tuple-element.258), channel_id=1, source_target_pairs={{0,1},{1,2},{2,3},{3,4},{4,5},{5,6},{6,7},{8,9},{9,10},{10,11},{11... | collective-permute-start | bytes 393224 | tf_op jit(solution)/shard_map/ppermute | solution.py:29
  16.1 768.5 %collective-permute-start = (f32[1,4,2048]{2,0,1:T(1,128)}, f32[1,4,2048]{2,0,1:T(1,128)S(1)}, u32[]{:S(2)}, u32[]{:S(2)}) collective-permute-start(f32[1,4,2048]{2,0,1:T(1,128)} %copy.88), channel_id=1, source_target_pairs={{8,0},{16,8},{24,16},{32,24},{40,32},{48,40},{56,48},{64,56},{72,6... | collective-permute-start | bytes 98312 | tf_op jit(solution)/shard_map/ppermute | solution.py:30
  21.2 763.3 %collective-permute-start.1 = (f32[1,4,2048]{2,0,1:T(1,128)}, f32[1,4,2048]{2,0,1:T(1,128)}, u32[]{:S(2)}, u32[]{:S(2)}) collective-permute-start(f32[1,4,2048]{2,0,1:T(1,128)} %copy.90), channel_id=1, source_target_pairs={{0,8},{8,16},{16,24},{24,32},{32,40},{40,48},{48,56},{56,64},{64,7... | collective-permute-start | bytes 98312 | tf_op jit(solution)/shard_map/ppermute | solution.py:29
  24.9 783.9 %all-to-all-start.2 = ((f32[64,1,512]{2,1,0:T(1,128)}), f32[64,1,512]{2,1,0:T(1,128)S(1)}, u32[]{:S(2)}, u32[]{:S(2)}) async-start(f32[64,1,512]{2,1,0:T(1,128)} %reshape.166), calls=%async_computation.2 | async-start | bytes 262144 | tf_op jit(solution)/shard_map/all_to_all | solution.py:47
  788.6 25.3 %copy-start.1 = (f32[16,4,2048]{2,1,0:T(4,128)S(1)}, f32[16,4,2048]{2,1,0:T(4,128)}, u32[]{:S(2)}) copy-start(f32[16,4,2048]{2,1,0:T(4,128)} %param.11) | copy-start | bytes 1572868
  791.1 22.8 %collective-permute-start.6 = (f32[16,1,2048]{2,0,1:T(8,128)}, f32[16,1,2048]{2,0,1:T(8,128)}, u32[]{:S(2)}, u32[]{:S(2)}) collective-permute-start(f32[16,1,2048]{2,0,1:T(8,128)} %get-tuple-element.249), channel_id=1, source_target_pairs={{1,0},{2,1},{3,2},{4,3},{5,4},{6,5},{7,6},{9,8},{10,9},{11,10},{12... | collective-permute-start | bytes 393224 | tf_op jit(solution)/shard_map/ppermute | solution.py:30
  792.4 21.5 %collective-permute-start.7 = (f32[16,1,2048]{2,0,1:T(8,128)}, f32[16,1,2048]{2,0,1:T(8,128)}, u32[]{:S(2)}, u32[]{:S(2)}) collective-permute-start(f32[16,1,2048]{2,0,1:T(8,128)} %get-tuple-element.250), channel_id=1, source_target_pairs={{0,1},{1,2},{2,3},{3,4},{4,5},{5,6},{6,7},{8,9},{9,10},{10,11},{11... | collective-permute-start | bytes 393224 | tf_op jit(solution)/shard_map/ppermute | solution.py:29
  802.2 9.2 collective-permute-start.4
  806.2 7.7 collective-permute-start.5
  816.1 22.8 %copy-start.5 = (f32[16,4,2048]{2,0,1:T(8,128)}, f32[16,4,2048]{2,0,1:T(8,128)S(1)}, u32[]{:S(2)}) copy-start(f32[16,4,2048]{2,0,1:T(8,128)S(1)} %get-tuple-element.179) | copy-start | bytes 1572868
  816.1 20.5 %copy-start.2 = (f32[16,4,2048]{2,1,0:T(4,128)S(1)}, f32[16,4,2048]{2,1,0:T(4,128)}, u32[]{:S(2)}) copy-start(f32[16,4,2048]{2,1,0:T(4,128)} %param.11) | copy-start | bytes 1572868
  816.5 20.2 %collective-permute-start.10 = (f32[16,1,2048]{2,0,1:T(8,128)S(1)}, f32[16,1,2048]{2,0,1:T(8,128)S(1)}, u32[]{:S(2)}, u32[]{:S(2)}) collective-permute-start(f32[16,1,2048]{2,0,1:T(8,128)S(1)} %get-tuple-element.241), channel_id=1, source_target_pairs={{1,0},{2,1},{3,2},{4,3},{5,4},{6,5},{7,6},{9,8},{10,9},{11,10},{12... | collective-permute-start | bytes 393224 | tf_op jit(solution)/shard_map/ppermute | solution.py:30
  817.9 18.8 %collective-permute-start.11 = (f32[16,1,2048]{2,0,1:T(8,128)S(1)}, f32[16,1,2048]{2,0,1:T(8,128)S(1)}, u32[]{:S(2)}, u32[]{:S(2)}) collective-permute-start(f32[16,1,2048]{2,0,1:T(8,128)S(1)} %get-tuple-element.242), channel_id=1, source_target_pairs={{0,1},{1,2},{2,3},{3,4},{4,5},{5,6},{6,7},{8,9},{9,10},{10,11},{11... | collective-permute-start | bytes 393224 | tf_op jit(solution)/shard_map/ppermute | solution.py:29
  826.4 4.9 collective-permute-start.8
  829.3 7.4 collective-permute-start.9
  853.0 55.3 %copy-start.25 = (f32[8]{0:T(128)S(1)}, f32[8]{0:T(128)}, u32[]{:S(2)}) copy-start(f32[8]{0:T(128)} %dynamic_slice.7) | copy-start | bytes 100
  890.1 18.8 %all-to-all-start = ((f32[64,1,512]{2,1,0:T(1,128)}), f32[64,1,512]{2,1,0:T(1,128)S(1)}, u32[]{:S(2)}, u32[]{:S(2)}) async-start(f32[64,1,512]{2,1,0:T(1,128)} %reshape.164), calls=%async_computation | async-start | bytes 262144 | tf_op jit(solution)/shard_map/all_to_all | solution.py:135
  918.8 17.5 %all-to-all-start.1 = ((f32[8,256,4,8]{1,3,2,0:T(8,128)}), f32[8,256,4,8]{1,3,2,0:T(8,128)S(1)}, u32[]{:S(2)}, u32[]{:S(2)}) async-start(f32[8,256,4,8]{1,3,2,0:T(8,128)} %broadcast_in_dim.89), calls=%async_computation.1 | async-start | bytes 524288 | tf_op jit(solution)/shard_map/all_to_all | solution.py:47
  951.1 26.5 %all-to-all-start.3 = ((f32[64,1,512]{2,1,0:T(1,128)}), f32[64,1,512]{2,1,0:T(1,128)S(1)}, u32[]{:S(2)}, u32[]{:S(2)}) async-start(f32[64,1,512]{2,1,0:T(1,128)} %reshape.168), calls=%async_computation.3 | async-start | bytes 262144 | tf_op jit(solution)/shard_map/all_to_all | solution.py:153
  960.8 39.7 %collective-permute-start.14 = (f32[16,1,2048]{2,0,1:T(8,128)}, f32[16,1,2048]{2,0,1:T(8,128)}, u32[]{:S(2)}, u32[]{:S(2)}) collective-permute-start(f32[16,1,2048]{2,0,1:T(8,128)} %get-tuple-element.233), channel_id=1, source_target_pairs={{1,0},{2,1},{3,2},{4,3},{5,4},{6,5},{7,6},{9,8},{10,9},{11,10},{12... | collective-permute-start | bytes 393224 | tf_op jit(solution)/shard_map/ppermute | solution.py:30
  962.1 38.5 %collective-permute-start.15 = (f32[16,1,2048]{2,0,1:T(8,128)}, f32[16,1,2048]{2,0,1:T(8,128)}, u32[]{:S(2)}, u32[]{:S(2)}) collective-permute-start(f32[16,1,2048]{2,0,1:T(8,128)} %get-tuple-element.234), channel_id=1, source_target_pairs={{0,1},{1,2},{2,3},{3,4},{4,5},{5,6},{6,7},{8,9},{9,10},{10,11},{11... | collective-permute-start | bytes 393224 | tf_op jit(solution)/shard_map/ppermute | solution.py:29
  971.2 29.3 %collective-permute-start.12 = (f32[1,4,2048]{2,0,1:T(1,128)}, f32[1,4,2048]{2,0,1:T(1,128)}, u32[]{:S(2)}, u32[]{:S(2)}) collective-permute-start(f32[1,4,2048]{2,0,1:T(1,128)} %get-tuple-element.236), channel_id=1, source_target_pairs={{8,0},{16,8},{24,16},{32,24},{40,32},{48,40},{56,48},{64,56},{72,6... | collective-permute-start | bytes 98312 | tf_op jit(solution)/shard_map/ppermute | solution.py:30
  975.0 25.5 %collective-permute-start.13 = (f32[1,4,2048]{2,0,1:T(1,128)}, f32[1,4,2048]{2,0,1:T(1,128)}, u32[]{:S(2)}, u32[]{:S(2)}) collective-permute-start(f32[1,4,2048]{2,0,1:T(1,128)} %get-tuple-element.235), channel_id=1, source_target_pairs={{0,8},{8,16},{16,24},{24,32},{32,40},{40,48},{48,56},{56,64},{64,7... | collective-permute-start | bytes 98312 | tf_op jit(solution)/shard_map/ppermute | solution.py:29
  1002.8 22.3 %collective-permute-start.18 = (f32[16,1,2048]{2,0,1:T(8,128)S(1)}, f32[16,1,2048]{2,0,1:T(8,128)S(1)}, u32[]{:S(2)}, u32[]{:S(2)}) collective-permute-start(f32[16,1,2048]{2,0,1:T(8,128)S(1)} %get-tuple-element.225), channel_id=1, source_target_pairs={{1,0},{2,1},{3,2},{4,3},{5,4},{6,5},{7,6},{9,8},{10,9},{11,10},{12... | collective-permute-start | bytes 393224 | tf_op jit(solution)/shard_map/ppermute | solution.py:30
  1004.1 21.0 %collective-permute-start.19 = (f32[16,1,2048]{2,0,1:T(8,128)S(1)}, f32[16,1,2048]{2,0,1:T(8,128)S(1)}, u32[]{:S(2)}, u32[]{:S(2)}) collective-permute-start(f32[16,1,2048]{2,0,1:T(8,128)S(1)} %get-tuple-element.226), channel_id=1, source_target_pairs={{0,1},{1,2},{2,3},{3,4},{4,5},{5,6},{6,7},{8,9},{9,10},{10,11},{11... | collective-permute-start | bytes 393224 | tf_op jit(solution)/shard_map/ppermute | solution.py:29
  1012.6 8.6 collective-permute-start.16
  1017.8 7.3 collective-permute-start.17
  1026.0 19.0 %collective-permute-start.22 = (f32[16,1,2048]{2,0,1:T(8,128)S(1)}, f32[16,1,2048]{2,0,1:T(8,128)S(1)}, u32[]{:S(2)}, u32[]{:S(2)}) collective-permute-start(f32[16,1,2048]{2,0,1:T(8,128)S(1)} %get-tuple-element.217), channel_id=1, source_target_pairs={{1,0},{2,1},{3,2},{4,3},{5,4},{6,5},{7,6},{9,8},{10,9},{11,10},{12... | collective-permute-start | bytes 393224 | tf_op jit(solution)/shard_map/ppermute | solution.py:30
  1027.3 17.7 %collective-permute-start.23 = (f32[16,1,2048]{2,0,1:T(8,128)S(1)}, f32[16,1,2048]{2,0,1:T(8,128)S(1)}, u32[]{:S(2)}, u32[]{:S(2)}) collective-permute-start(f32[16,1,2048]{2,0,1:T(8,128)S(1)} %get-tuple-element.218), channel_id=1, source_target_pairs={{0,1},{1,2},{2,3},{3,4},{4,5},{5,6},{6,7},{8,9},{9,10},{10,11},{11... | collective-permute-start | bytes 393224 | tf_op jit(solution)/shard_map/ppermute | solution.py:29
  1035.8 4.4 collective-permute-start.20
  1037.7 7.3 collective-permute-start.21
  (22 other events, 223.6 us)
where the time goes:
time: 1070 us; the launch traced here: 1050 us
  loops' own time  487 us (46%)
  other arithmetic  252 us (24%)
  starting transfers between devices  127 us (12%)
  local copies, waits for them, and re-layouts  71.7 us (7%)
  blocking collectives  52.2 us (5%)
  waiting for transfers between devices  28.4 us (3%)
  matrix products  27.6 us (3%)
    another operation x1, loops' own time, legendre(): lax.scan(step, start, jnp.arange(count, dtype=jnp.float32), unroll=16)  487 us
    mul x80, other arithmetic, step(): return ((current, nextone), current * jnp.sqrt(degree + 0.5))  224 us
    ppermute x12, starting transfers between devices, extended(): lax.ppermute(last, axis, up)  67.2 us
    psum x5, blocking collectives, over_axes(): return functools.reduce(lax.psum, axes, x)  52.2 us
    ppermute x12, starting transfers between devices, extended(): lax.ppermute(first, axis, [(b, a) for a, b in up])  30.2 us
  transfers between devices with their start and end apart: 28, of which 5 were waited for; matrix products, arithmetic and copies ran while one was open for 29% of the time, Pallas kernels for 0%

commit v1 on v0

v1 whole, which is shorter than its diff:
```python
import numpy as np
import jax
import jax.numpy as jnp
import ml_dtypes
from jax import lax
from jax.experimental import pallas as pl
from jax.experimental.pallas import tpu as pltpu
from jax.sharding import Mesh
from jax.sharding import PartitionSpec as P

LAT = ("lat_0", "lat_1", "lat_2")
RAD = ("rad_0", "rad_1")
ALL = LAT + RAD

NLON, NLAT, NR, MODES, NDEG = 2048, 1024, 32, 256, 256
DEV, NI, NB, NJ, NK = 512, 64, 8, 16, 4
HALF = NLON // 2
RIN, ROUT = 9, 5
LOAD, SHIFT, RELAX, COUPLE = 0.5, 0.5, 0.8, 2.0
DIAG = 6.0 + SHIFT
F32, BF16 = jnp.float32, jnp.bfloat16


def split_np(x):
    hi = x.astype(np.float32).astype(ml_dtypes.bfloat16)
    lo = (x - hi.astype(np.float64)).astype(np.float32).astype(ml_dtypes.bfloat16)
    return hi, lo


def order_tables():
    kind = np.zeros((2, 2, DEV), np.int64)
    order = np.zeros((2, 2, DEV), np.int64)
    for par in range(2):
        high = [(k, c) for c in range(MODES + par, HALF, 2) for k in (0, 1)]
        rest = iter(high)
        for kk in range(2):
            for p in range(DEV):
                if kk == 0 and p % 2 == par:
                    k, c = (0, p) if p < MODES else (1, p - MODES)
                    if k == 1 and c == 0:
                        k, c = 0, HALF
                else:
                    k, c = next(rest)
                kind[par, kk, p], order[par, kk, p] = k, c
    return kind, order


def fourier_tables():
    kind, order = order_tables()
    l = np.arange(HALF)
    phase = (order[..., None] * l) % NLON
    angle = phase * (2.0 * np.pi / NLON)
    value = np.where(kind[..., None] == 0, np.cos(angle), np.sin(angle)) * np.sqrt(2.0 / NLON)
    value = np.where((order % HALF == 0)[..., None], value * np.sqrt(0.5), value)
    eigen = 2.0 * np.cos(order * (2.0 * np.pi / NLON))
    gain = (1.0 - RELAX) + RELAX / DIAG * eigen
    hi, lo = split_np(value)
    return hi, lo, np.ascontiguousarray(gain.transpose(2, 1, 0).reshape(DEV * 4)).astype(np.float32)


def legendre_tables():
    theta = (np.arange(NLAT) + 0.5) * (np.pi / NLAT)
    mu = np.cos(theta)
    rows = np.zeros((NDEG, NLAT))
    before, current = np.zeros(NLAT), np.ones(NLAT)
    for n in range(NDEG):
        rows[n] = current * np.sqrt(n + 0.5)
        before, current = current, ((2 * n + 1) * mu * current - n * before) / (n + 1)
    weight = np.pi / NLAT * np.sin(theta)
    rows = rows.reshape(NI, 4, NLAT).transpose(1, 0, 2).reshape(NDEG, NI, NJ)
    rows = rows.transpose(0, 2, 1).reshape(NDEG, NLAT)
    weight = weight.reshape(NI, NJ).T.reshape(1, NLAT)
    hi, lo = split_np(rows)
    return hi, lo, weight.astype(np.float32)


def split(x):
    hi = x.astype(BF16)
    return hi, (x - hi.astype(F32)).astype(BF16)


def dot_nt(a, b):
    return lax.dot_general(a, b, (((1,), (1,)), ((), ())), preferred_element_type=F32)


def dot_nn(a, b):
    return lax.dot_general(a, b, (((1,), (0,)), ((), ())), preferred_element_type=F32)


PB = 128


def forward_kernel(u_ref, q_ref, ice_ref, mat_ref, ker_ref, th_ref, tl_ref, a_ref, x_ref, w_ref):
    @pl.when(pl.program_id(0) == 0)
    def _():
        for f, ref in ((0, u_ref), (1, q_ref)):
            for j in range(NJ):
                w_ref[pl.ds(64 * f + 4 * j, 4), :] = ref[j]
        low, high = w_ref[:, :HALF], w_ref[:, HALF:]
        ice = ice_ref[...].astype(F32)
        il, ih = ice[:, :HALF], ice[:, HALF:]
        x_ref[...] = jnp.zeros(x_ref.shape, BF16)
        for k2 in range(2):
            part = low + high if k2 == 0 else low - high
            ipart = il + ih if k2 == 0 else il - ih
            ph, plo = split(part)
            for kk in range(2):
                x_ref[k2, kk, 0:128, :] = plo
                x_ref[k2, kk, 128:256, :] = ph
                x_ref[k2, kk, pl.ds(256 + (kk * 2 + k2) * NJ, NJ), :] = ipart.astype(BF16)

    lane = lax.broadcasted_iota(jnp.int32, (PB, 128), 1)
    first = lane < 64
    extra = jnp.broadcast_to(mat_ref[...], (PB, 128))
    for kk in range(2):
        main = []
        for k2 in range(2):
            x = x_ref[k2, kk]
            r1 = dot_nt(th_ref[k2, kk], x)
            r2 = dot_nt(tl_ref[k2, kk], x[128:])
            main.append(r1[:, 128:256] + (r1[:, :128] + r2[:, :128]))
            extra = extra + (r1[:, 256:] + r2[:, 128:])
        even, odd = main
        a_ref[pl.ds(kk, PB, stride=RIN), :] = jnp.where(first, even, pltpu.roll(odd, 64, 1))
        a_ref[pl.ds(2 + kk, PB, stride=RIN), :] = jnp.where(first, pltpu.roll(even, 64, 1), odd)
    a_ref[pl.ds(4, PB, stride=RIN), :] = extra
    for nn in range(4):
        a_ref[pl.ds(5 + nn, PB, stride=RIN), :] = jnp.broadcast_to(ker_ref[pl.ds(nn, 1), :], (PB, 128))


def forward(u, q, ice, mat, ker, th, tl):
    whole = lambda shape: pl.BlockSpec(shape, lambda g: (0,) * len(shape))
    table = pl.BlockSpec((2, 2, PB, HALF), lambda g: (0, 0, g, 0))
    return pl.pallas_call(
        forward_kernel,
        grid=(DEV // PB,),
        in_specs=[
            whole((NJ, NK, NLON)),
            whole((NJ, NK, NLON)),
            whole((NJ, NLON)),
            whole((1, 128)),
            whole((4, 128)),
            table,
            table,
        ],
        out_specs=pl.BlockSpec((PB * RIN, 128), lambda g: (g, 0)),
        out_shape=jax.ShapeDtypeStruct((DEV * RIN, 128), F32),
        scratch_shapes=[pltpu.VMEM((2, 2, 384, HALF), BF16), pltpu.VMEM((128, NLON), F32)],
        compiler_params=pltpu.CompilerParams(vmem_limit_bytes=48 << 20),
        name="forward",
    )(u, q, ice, mat, ker, th, tl)


def middle_kernel(
    dev_ref, gain_ref, mu_ref, dec_ref, con_ref, b_ref, ph_ref, pl_ref, wt_ref, o_ref,
    u_ref, q_ref, s_ref, st_ref, dc_ref, g_ref, r_ref, z_ref, rt_ref,
):
    p = dev_ref[0]
    par = p % 2
    shape = (NI, 128)
    lane = lax.broadcasted_iota(jnp.int32, shape, 1)
    row = lax.broadcasted_iota(jnp.int32, shape, 0)
    r = lane & 3
    j = (lane >> 2) & 15
    first = lane < 64
    rp = (lane & ~3) | ((lane + 1) & 3)
    rm = (lane & ~3) | ((lane + 3) & 3)
    jp = (lane & 64) | ((lane + 4) & 63)
    jm = (lane & 64) | ((lane + 60) & 63)

    def take(x, index):
        return jnp.take_along_axis(x, index, axis=1)

    zero = jnp.zeros(shape, F32)
    for buf in range(2):
        for kk in range(2):
            u_ref[buf, kk, 0] = zero
            u_ref[buf, kk, NB + 1] = zero
    for b in range(NB):
        extra = b_ref[pl.ds(b * RIN + 4, NI, stride=NB * RIN), :]
        mat = take(extra, 64 + (lane & 63))

        def look(ref):
            out = jnp.full(shape, ref[0], F32)
            for m in range(1, 8):
                out = jnp.where(mat == float(m), ref[m], out)
            return out

        stiff = look(mu_ref)
        st_ref[b] = stiff
        dc_ref[b] = look(dec_ref)
        r_ref[b] = look(con_ref)
        g_ref[b] = (RELAX / DIAG) / stiff
        layer = (r + (4 * b + 1)).astype(F32) * (LOAD / NR)
        for kk in range(2):
            s_ref[kk, b] = take(extra, kk * 32 + (lane >> 2)) * layer
            u_ref[0, kk, b + 1] = b_ref[pl.ds(b * RIN + kk, NI, stride=NB * RIN), :]
            q_ref[kk, b] = b_ref[pl.ds(b * RIN + 2 + kk, NI, stride=NB * RIN), :]

    gains = [jnp.where(first, gain_ref[4 * p + 2 * kk], gain_ref[4 * p + 2 * kk + 1]) for kk in range(2)]

    def sweep(src, dst):
        for kk in range(2):
            for b in range(NB):
                uc = u_ref[src, kk, b + 1]
                up = u_ref[src, kk, b + 2]
                dn = u_ref[src, kk, b]
                ip = jnp.where(row == NI - 1, 0.0, pltpu.roll(uc, NI - 1, 0))
                im = jnp.where(row == 0, 0.0, pltpu.roll(uc, 1, 0))
                beside = take(jnp.where(r == 0, up, uc), rp) + take(jnp.where(r == 3, dn, uc), rm)
                beside = beside + take(jnp.where(j == 0, ip, uc), jp) + take(jnp.where(j == 15, im, uc), jm)
                q = q_ref[kk, b]
                un = gains[kk] * uc + g_ref[b] * (s_ref[kk, b] - q) + (RELAX / DIAG) * beside
                u_ref[dst, kk, b + 1] = un
                q_ref[kk, b] = dc_ref[b] * q + st_ref[b] * (un - uc)

    def three(start):
        def body(step, carry):
            src = (start + step) % 2
            sweep(src, 1 - src)
            return carry

        lax.fori_loop(0, 3, body, 0)

    three(0)
    for h in range(NB // 2):
        pair = [r_ref[2 * h + t] * u_ref[1, 0, 2 * h + t + 1] for t in range(2)]
        rt_ref[:, 128 * h : 128 * h + 128] = jnp.concatenate(pair, axis=0).T
    kept = rt_ref[pl.ds(pl.multiple_of(64 * par, 64), 64), :]
    for jj in range(NJ):
        for b in range(NB):
            z_ref[4 * b : 4 * b + 4, 64 * jj : 64 * jj + 64] = kept[4 * jj : 4 * jj + 4, 64 * b : 64 * b + 64]
    z = z_ref[...]
    mean = jnp.sum(z) * (1.0 / (NLAT * NR))
    z = z - jnp.where(p == 0, mean, 0.0)
    z = z * wt_ref[...]
    z4 = jnp.concatenate([z, z, z, z], axis=0)
    zh, zl = split(z4)
    ph, plo = ph_ref[...], pl_ref[...]
    coef = dot_nt(ph, zh) + (dot_nt(ph, zl) + dot_nt(plo, zh))
    lane1 = lax.broadcasted_iota(jnp.int32, (128, 128), 1)
    sub1 = lax.broadcasted_iota(jnp.int32, (128, 128), 0)
    phi = jnp.zeros((NDEG, 128), F32)
    for b in range(NB):
        prod = jnp.concatenate(
            [
                b_ref[pl.ds(b * RIN + 5 + nn, NI, stride=NB * RIN), :] * coef[64 * nn : 64 * nn + 64]
                for nn in range(4)
            ],
            axis=0,
        )
        pick = (lane1 == (sub1 >> 5) + 4 * b).astype(BF16)
        hi, lo = split(prod)
        phi = phi + (dot_nn(hi, pick) + dot_nn(lo, pick))
    factor = jnp.where(p == 0, 2.0, jnp.where(p == MODES, 0.0, 1.0))
    phi_t = (phi * factor).T[0:NR]
    fh, fl = split(phi_t)
    pot = dot_nn(fh, ph) + (dot_nn(fl, ph) + dot_nn(fh, plo))
    rt_ref[...] = jnp.zeros(rt_ref.shape, F32)
    for jj in range(NJ):
        for b in range(NB):
            z_ref2 = pot[4 * b : 4 * b + 4, 64 * jj : 64 * jj + 64]
            kept_ref = rt_ref.at[pl.ds(pl.multiple_of(64 * par, 64), 64), :]
            kept_ref[4 * jj : 4 * jj + 4, 64 * b : 64 * b + 64] = z_ref2
    for h in range(NB // 2):
        back = rt_ref[:, 128 * h : 128 * h + 128].T
        for t in range(2):
            b = 2 * h + t
            piece = back[64 * t : 64 * t + 64]
            o_ref[pl.ds(b * ROUT + 4, NI, stride=NB * ROUT), :] = piece
            s_ref[0, b] = s_ref[0, b] + COUPLE * piece
    three(1)
    for b in range(NB):
        for kk in range(2):
            o_ref[pl.ds(b * ROUT + kk, NI, stride=NB * ROUT), :] = u_ref[0, kk, b + 1]
            o_ref[pl.ds(b * ROUT + 2 + kk, NI, stride=NB * ROUT), :] = q_ref[kk, b]


def middle(dev, gain, mu, dec, con, b, ph, plo, wt):
    smem = pl.BlockSpec(memory_space=pltpu.SMEM)
    vmem = pl.BlockSpec(memory_space=pltpu.VMEM)
    field = (NB, NI, 128)
    return pl.pallas_call(
        middle_kernel,
        in_specs=[smem] * 5 + [vmem] * 4,
        out_specs=vmem,
        out_shape=jax.ShapeDtypeStruct((DEV * ROUT, 128), F32),
        scratch_shapes=[
            pltpu.VMEM((2, 2, NB + 2, NI, 128), F32),
            pltpu.VMEM((2, *field), F32),
            pltpu.VMEM((2, *field), F32),
            pltpu.VMEM(field, F32),
            pltpu.VMEM(field, F32),
            pltpu.VMEM(field, F32),
            pltpu.VMEM(field, F32),
            pltpu.VMEM((NR, NLAT), F32),
            pltpu.VMEM((128, DEV), F32),
        ],
        compiler_params=pltpu.CompilerParams(vmem_limit_bytes=48 << 20),
        name="middle",
    )(dev, gain, mu, dec, con, b, ph, plo, wt)


LB = 256


def inverse_kernel(b_ref, th_ref, tl_ref, u_ref, q_ref, p_ref, y_ref):
    @pl.when(pl.program_id(0) == 0)
    def _():
        for f in range(3):
            for kk in range(2):
                if f == 2 and kk == 1:
                    continue
                rows = b_ref[pl.ds(4 if f == 2 else 2 * f + kk, DEV, stride=ROUT), :].T
                hi, lo = split(rows)
                for k2 in range(2):
                    y_ref[k2, 64 * f : 64 * f + 64, DEV * kk : DEV * kk + DEV] = hi[64 * k2 : 64 * k2 + 64]
                    y_ref[k2, 192 + 64 * f : 256 + 64 * f, DEV * kk : DEV * kk + DEV] = lo[64 * k2 : 64 * k2 + 64]
        for k2 in range(2):
            for base in (128, 320):
                y_ref[k2, base : base + 64, DEV:] = jnp.zeros((64, DEV), BF16)

    halves = []
    for k2 in range(2):
        th = th_ref[k2].reshape(2 * DEV, LB)
        tl = tl_ref[k2].reshape(2 * DEV, LB)
        y = y_ref[k2]
        r1 = dot_nn(y, th)
        halves.append(r1[:192] + (r1[192:] + dot_nn(y[:192], tl)))
    even, odd = halves
    start = pl.multiple_of(pl.program_id(0) * LB, LB)
    for base, value in ((0, even + odd), (HALF, even - odd)):
        for f, ref in enumerate((u_ref, q_ref, p_ref)):
            for j in range(NJ):
                ref[j, :, pl.ds(base + start, LB)] = value[64 * f + 4 * j : 64 * f + 4 * j + 4]


def inverse(b, th, tl):
    whole = lambda shape: pl.BlockSpec(shape, lambda g: (0,) * len(shape))
    table = pl.BlockSpec((2, 2, DEV, LB), lambda g: (0, 0, 0, g))
    shape = (NJ, NK, NLON)
    return pl.pallas_call(
        inverse_kernel,
        grid=(HALF // LB,),
        in_specs=[whole((DEV * ROUT, 128)), table, table],
        out_specs=[whole(shape)] * 3,
        out_shape=[jax.ShapeDtypeStruct(shape, F32)] * 3,
        scratch_shapes=[pltpu.VMEM((2, 384, HALF), BF16)],
        compiler_params=pltpu.CompilerParams(vmem_limit_bytes=48 << 20),
        name="inverse",
    )(b, th, tl)


def exchange(x, rows):
    x = x.reshape(DEV, rows * 128)
    x = lax.all_to_all(x, ALL, split_axis=0, concat_axis=0, tiled=True)
    return x.reshape(DEV * rows, 128)


def solution(mesh):
    torus = Mesh(mesh.devices.reshape(4, 8, 2, 4, 2), ALL)
    th_np, tl_np, gain_np = fourier_tables()
    ph_np, pl_np, wt_np = legendre_tables()

    def per_device(
        displacement, memory, ice_class, material, mu_table, decay_table, contrast_table, gravity_kernel
    ):
        th, tl = jnp.asarray(th_np), jnp.asarray(tl_np)
        mat = jnp.pad(material.reshape(1, 64).astype(F32), ((0, 0), (64, 0)))
        ker = gravity_kernel.reshape(4, 128)
        dev = lax.axis_index(ALL).reshape(1)
        packed = forward(displacement, memory, ice_class, mat, ker, th, tl)
        arrived = exchange(packed, RIN)
        moved = middle(
            dev, jnp.asarray(gain_np), mu_table, decay_table, contrast_table, arrived,
            jnp.asarray(ph_np), jnp.asarray(pl_np), jnp.asarray(wt_np),
        )
        returned = exchange(moved, ROUT)
        return tuple(inverse(returned, th, tl))

    in_specs = (
        P(LAT, RAD, None),
        P(LAT, RAD, None),
        P(LAT, None),
        P(LAT, RAD),
        P(),
        P(),
        P(),
        P(LAT, RAD, None),
    )
    out_specs = (P(LAT, RAD, None), P(LAT, RAD, None), P(LAT, RAD, None))
    return jax.shard_map(per_device, mesh=torus, in_specs=in_specs, out_specs=out_specs, check_vma=False)
```

time: 1070 us -> 166 us (0.16)
  the two profiles are of different devices: /device:TPU:64 before, /device:TPU:1 now
where the time goes in v1:
time: 166 us
  waiting for transfers between devices  61.2 us (37%)
  blocking collectives  47.3 us (28%)
  Pallas kernels  29.6 us (18%)
  starting transfers between devices  22.2 us (13%)
  local copies, waits for them, and re-layouts  4.06 us (2%)
    all_to_all x1, waiting for transfers between devices, exchange(): x = lax.all_to_all(x, ALL, split_axis=0, concat_axis=0, tiled=True)  61.2 us
    all_to_all x1, blocking collectives, exchange(): x = lax.all_to_all(x, ALL, split_axis=0, concat_axis=0, tiled=True)  47.3 us
    all_to_all x1, starting transfers between devices, exchange(): x = lax.all_to_all(x, ALL, split_axis=0, concat_axis=0, tiled=True)  22.2 us
    pallas_call x1, Pallas kernels, middle(): pl.pallas_call(middle_kernel, in_specs=[smem] * 5 + [vmem] * 4, out_specs...  12.6 us
    pallas_call x1, Pallas kernels, forward(): pl.pallas_call(forward_kernel, grid=(DEV // PB,), in_specs=[whole((NJ, NK...  10.2 us
    pallas_call x1, Pallas kernels, inverse(): pl.pallas_call(inverse_kernel, grid=(HALF // LB,), in_specs=[whole((DEV *...  6.84 us
  transfers between devices with their start and end apart: 1, of which 1 were waited for; matrix products, arithmetic and copies ran while one was open for 0% of the time, Pallas kernels for 0%

profile of v1, /device:TPU:1, one launch (start us, length us, event | category | flops | bytes accessed | tf_op | source)
XLA Modules:
  0.0 165.8 jit_solution(3496447387278953999)
XLA Ops:
  0.6 0.7 convert_element_type.16
  1.3 0.8 reshape.43.ker_ref
  2.1 0.1 copy.19
  2.2 0.1 convert_element_type.17
  2.3 0.1 pad.4.mat_ref
  2.3 0.0 copy-start.1
  2.3 1.0 copy-done.1
  3.4 0.0 copy-start.2
  3.4 1.0 copy-done.2
  4.4 0.0 copy-start.5
  4.4 0.9 copy-done.5
  5.3 10.2 %forward.1 = f32[4608,128]{1,0:T(8,128)} custom-call(f32[16,4,2048]{2,1,0:T(4,128)S(1)} %copy-done.1, f32[16,4,2048]{2,1,0:T(4,128)S(1)} %copy-done.2, s32[16,2048]{1,0:T(8,128)S(1)} %copy-done.5, f32[1,128]{1,0:T(1,128)S(1)} %pad.4.mat_ref, f32[4,128]{1,0:T(4,128)S(1)} %reshape.43.ker_ref, bf16[2,2,512,1024]{3,2,1,0:T(8,128)(2,1)} %constant.42.clone.th_ref, ...), custom_call_target="tpu_custom_call" | custom-call | tf_op jit(solution)/shard_map/forward/pallas_call | solution.py:134
  15.5 0.0 copy-start.3
  15.5 0.0 copy-start.4
  15.5 0.0 copy-start.7
  15.5 0.0 copy-start.8
  15.5 0.0 copy-start.9
  15.6 0.0 copy-start.10
  15.6 22.2 %all-to-all-start = ((f32[512,1,1152]{2,1,0:T(1,128)}), f32[512,1,1152]{2,1,0:T(1,128)S(1)}, u32[]{:S(2)}, u32[]{:S(2)}) async-start(f32[512,1,1152]{2,1,0:T(1,128)} %bitcast.1), calls=%async_computation | async-start | bytes 4718592 | tf_op jit(solution)/shard_map/all_to_all | solution.py:356
  37.8 61.2 %all-to-all-done = f32[512,1,1152]{2,1,0:T(1,128)S(1)} async-done(((f32[512,1,1152]{2,1,0:T(1,128)}), f32[512,1,1152]{2,1,0:T(1,128)S(1)}, u32[]{:S(2)}, u32[]{:S(2)}) %all-to-all-start) | async-done | bytes 2359328 | tf_op jit(solution)/shard_map/all_to_all | solution.py:356
  99.0 0.0 copy-done.3
  99.0 0.0 copy-done.4
  99.0 0.0 copy-done.6
  99.0 0.0 copy-done.7
  99.0 0.0 copy-done.8
  99.0 0.0 copy-done.9
  99.0 0.0 copy-done.10
  99.1 0.0 copy-start
  99.1 12.6 %middle.1 = f32[2560,128]{1,0:T(8,128)S(1)} custom-call(s32[1]{0:T(128)} %bitcast.dev_ref, f32[2048]{0:T(1024)S(1)} %copy-done.6, f32[8]{0:T(128)S(1)} %copy-done.8, f32[8]{0:T(128)S(1)} %copy-done.9, f32[8]{0:T(128)S(1)} %copy-done.10, f32[4608,128]{1,0:T(8,128)S(1)} %bitcast.5, bf16[256,1024]{1,0:T(8,128)(2,1)S(1)} %copy-done.4, ...), custom_call_target="tpu_custom_call" | custom-call | tf_op jit(solution)/shard_map/middle/pallas_call | solution.py:283
  111.7 47.3 %all_to_all.18 = f32[512,1,640]{2,1,0:T(1,128)S(1)} all-to-all(f32[512,1,640]{2,1,0:T(1,128)S(1)} %bitcast.6), channel_id=1, replica_groups=mesh['lat_0'=4,'lat_1'=8,'lat_2'=2,'rad_0'=4,'rad_1'=2] {'lat_0','lat_1'..., dimensions={0} | all-to-all | bytes 2621440 | tf_op jit(solution)/shard_map/all_to_all | solution.py:356
  159.0 0.0 copy-done
  159.0 6.8 %inverse.1 = (f32[16,4,2048]{2,1,0:T(4,128)}, f32[16,4,2048]{2,1,0:T(4,128)}, f32[16,4,2048]{2,1,0:T(4,128)}) custom-call(f32[2560,128]{1,0:T(8,128)S(1)} %bitcast.7, bf16[2,2,512,1024]{3,2,1,0:T(8,128)(2,1)S(1)} %copy-done, bf16[2,2,512,1024]{3,2,1,0:T(8,128)(2,1)} %constant.43.clone.tl_ref), custom_call_target="tpu_custom_call" | custom-call | tf_op jit(solution)/shard_map/inverse/pallas_call | solution.py:342
  (1 shorter events, 0.0 us)
Async XLA Ops:
  2.3 1.0 copy-start.1
  3.4 1.0 copy-start.2
  4.4 0.9 copy-start.5
  15.5 83.5 %copy-start.3 = (bf16[256,1024]{1,0:T(8,128)(2,1)S(1)}, bf16[256,1024]{1,0:T(8,128)(2,1)}, u32[]{:S(2)}) copy-start(bf16[256,1024]{1,0:T(8,128)(2,1)} %constant.46.clone.pl_ref) | copy-start | bytes 1572868
  15.5 83.5 %copy-start.4 = (bf16[256,1024]{1,0:T(8,128)(2,1)S(1)}, bf16[256,1024]{1,0:T(8,128)(2,1)}, u32[]{:S(2)}) copy-start(bf16[256,1024]{1,0:T(8,128)(2,1)} %constant.45.clone.ph_ref) | copy-start | bytes 1572868
  15.5 83.5 %copy-start.6 = (f32[2048]{0:T(1024)S(1)}, f32[2048]{0:T(1024)}, u32[]{:S(2)}) copy-start(f32[2048]{0:T(1024)} %constant.44.clone.gain_ref) | copy-start | bytes 24580
  15.5 83.5 %copy-start.7 = (f32[1,1024]{1,0:T(1,128)S(1)}, f32[1,1024]{1,0:T(1,128)}, u32[]{:S(2)}) copy-start(f32[1,1024]{1,0:T(1,128)} %constant.47.clone.wt_ref) | copy-start | bytes 12292
  15.5 83.5 %copy-start.8 = (f32[8]{0:T(128)S(1)}, f32[8]{0:T(128)}, u32[]{:S(2)}) copy-start(f32[8]{0:T(128)} %mu_ref.1) | copy-start | bytes 100
  15.5 83.5 %copy-start.9 = (f32[8]{0:T(128)S(1)}, f32[8]{0:T(128)}, u32[]{:S(2)}) copy-start(f32[8]{0:T(128)} %dec_ref.1) | copy-start | bytes 100
  15.6 83.5 %copy-start.10 = (f32[8]{0:T(128)S(1)}, f32[8]{0:T(128)}, u32[]{:S(2)}) copy-start(f32[8]{0:T(128)} %con_ref.1) | copy-start | bytes 100
  15.6 83.4 %all-to-all-start = ((f32[512,1,1152]{2,1,0:T(1,128)}), f32[512,1,1152]{2,1,0:T(1,128)S(1)}, u32[]{:S(2)}, u32[]{:S(2)}) async-start(f32[512,1,1152]{2,1,0:T(1,128)} %bitcast.1), calls=%async_computation | async-start | bytes 4718592 | tf_op jit(solution)/shard_map/all_to_all | solution.py:356
  99.1 59.9 %copy-start = (bf16[2,2,512,1024]{3,2,1,0:T(8,128)(2,1)S(1)}, bf16[2,2,512,1024]{3,2,1,0:T(8,128)(2,1)}, u32[]{:S(2)}) copy-start(bf16[2,2,512,1024]{3,2,1,0:T(8,128)(2,1)} %constant.42.clone.th_ref) | copy-start | bytes 12582916

commit v2 on v1

--- a/solution.py
+++ b/solution.py
@@ -15,7 +15,7 @@
 NLON, NLAT, NR, MODES, NDEG = 2048, 1024, 32, 256, 256
 DEV, NI, NB, NJ, NK = 512, 64, 8, 16, 4
 HALF = NLON // 2
-RIN, ROUT = 9, 5
+RIN, ROUT = 7, 5
 LOAD, SHIFT, RELAX, COUPLE = 0.5, 0.5, 0.8, 2.0
 DIAG = 6.0 + SHIFT
 F32, BF16 = jnp.float32, jnp.bfloat16
@@ -87,95 +87,107 @@
     return lax.dot_general(a, b, (((1,), (0,)), ((), ())), preferred_element_type=F32)
 
 
-PB = 128
-
-
-def forward_kernel(u_ref, q_ref, ice_ref, mat_ref, ker_ref, th_ref, tl_ref, a_ref, x_ref, w_ref):
-    @pl.when(pl.program_id(0) == 0)
+def forward_kernel(
+    u_hbm, q_hbm, ice_hbm, mat_ref, ker_ref, th_ref, tl_ref, a_ref, x_ref, w_ref, f_ref, ice_ref, even_ref, extra_ref, sem
+):
+    g = pl.program_id(0)
+    kk, k2 = g // 2, g % 2
+
+    @pl.when(g == 0)
     def _():
-        for f, ref in ((0, u_ref), (1, q_ref)):
+        copies = [
+            pltpu.make_async_copy(u_hbm, f_ref.at[0], sem.at[0]),
+            pltpu.make_async_copy(q_hbm, f_ref.at[1], sem.at[1]),
+            pltpu.make_async_copy(ice_hbm, ice_ref, sem.at[2]),
+        ]
+        for copy in copies:
+            copy.start()
+        x_ref[:, :, 256:, :] = jnp.zeros((2, 2, 128, HALF), BF16)
+        peer = lax.broadcasted_iota(jnp.int32, (DEV, 128), 0)
+        core = (peer >> 3) & 1
+        for t in range(2):
+            mine = jnp.where(core == 0, ker_ref[pl.ds(t, 1), :], ker_ref[pl.ds(2 + t, 1), :])
+            a_ref[pl.ds(5 + t, DEV, stride=RIN), :] = mine
+        for f in range(2):
+            copies[f].wait()
             for j in range(NJ):
-                w_ref[pl.ds(64 * f + 4 * j, 4), :] = ref[j]
+                w_ref[pl.ds(64 * f + 4 * j, 4), :] = f_ref[f, j]
+        copies[2].wait()
         low, high = w_ref[:, :HALF], w_ref[:, HALF:]
         ice = ice_ref[...].astype(F32)
         il, ih = ice[:, :HALF], ice[:, HALF:]
-        x_ref[...] = jnp.zeros(x_ref.shape, BF16)
-        for k2 in range(2):
-            part = low + high if k2 == 0 else low - high
-            ipart = il + ih if k2 == 0 else il - ih
+        for par in range(2):
+            part = low + high if par == 0 else low - high
+            ipart = il + ih if par == 0 else il - ih
             ph, plo = split(part)
-            for kk in range(2):
-                x_ref[k2, kk, 0:128, :] = plo
-                x_ref[k2, kk, 128:256, :] = ph
-                x_ref[k2, kk, pl.ds(256 + (kk * 2 + k2) * NJ, NJ), :] = ipart.astype(BF16)
-
-    lane = lax.broadcasted_iota(jnp.int32, (PB, 128), 1)
-    first = lane < 64
-    extra = jnp.broadcast_to(mat_ref[...], (PB, 128))
-    for kk in range(2):
-        main = []
-        for k2 in range(2):
-            x = x_ref[k2, kk]
-            r1 = dot_nt(th_ref[k2, kk], x)
-            r2 = dot_nt(tl_ref[k2, kk], x[128:])
-            main.append(r1[:, 128:256] + (r1[:, :128] + r2[:, :128]))
-            extra = extra + (r1[:, 256:] + r2[:, 128:])
-        even, odd = main
-        a_ref[pl.ds(kk, PB, stride=RIN), :] = jnp.where(first, even, pltpu.roll(odd, 64, 1))
-        a_ref[pl.ds(2 + kk, PB, stride=RIN), :] = jnp.where(first, pltpu.roll(even, 64, 1), odd)
-    a_ref[pl.ds(4, PB, stride=RIN), :] = extra
-    for nn in range(4):
-        a_ref[pl.ds(5 + nn, PB, stride=RIN), :] = jnp.broadcast_to(ker_ref[pl.ds(nn, 1), :], (PB, 128))
+            for slot in range(2):
+                x_ref[slot, par, 0:128, :] = plo
+                x_ref[slot, par, 128:256, :] = ph
+                x_ref[slot, par, pl.ds(256 + (slot * 2 + par) * NJ, NJ), :] = ipart.astype(BF16)
+        extra_ref[...] = jnp.broadcast_to(mat_ref[...], (DEV, 128))
+
+    first = lax.broadcasted_iota(jnp.int32, (DEV, 128), 1) < 64
+    x = x_ref[kk, k2]
+    r1 = dot_nt(th_ref[0, 0], x)
+    r2 = dot_nt(tl_ref[0, 0], x[128:])
+    main = r1[:, 128:256] + (r1[:, :128] + r2[:, :128])
+    extra_ref[...] += r1[:, 256:] + r2[:, 128:]
+
+    @pl.when(k2 == 0)
+    def _():
+        even_ref[...] = main
+
+    @pl.when(k2 == 1)
+    def _():
+        even = even_ref[...]
+        a_ref[pl.ds(kk, DEV, stride=RIN), :] = jnp.where(first, even, pltpu.roll(main, 64, 1))
+        a_ref[pl.ds(2 + kk, DEV, stride=RIN), :] = jnp.where(first, pltpu.roll(even, 64, 1), main)
+
+    @pl.when(g == 3)
+    def _():
+        a_ref[pl.ds(4, DEV, stride=RIN), :] = extra_ref[...]
 
 
 def forward(u, q, ice, mat, ker, th, tl):
     whole = lambda shape: pl.BlockSpec(shape, lambda g: (0,) * len(shape))
-    table = pl.BlockSpec((2, 2, PB, HALF), lambda g: (0, 0, g, 0))
+    hbm = pl.BlockSpec(memory_space=pltpu.MemorySpace.HBM)
+    u, q, ice = (pltpu.with_memory_space_constraint(x, pltpu.MemorySpace.HBM) for x in (u, q, ice))
+    th, tl = (pltpu.with_memory_space_constraint(x, pltpu.MemorySpace.HBM) for x in (th, tl))
+    table = pl.BlockSpec((1, 1, DEV, HALF), lambda g: (g % 2, g // 2, 0, 0))
     return pl.pallas_call(
         forward_kernel,
-        grid=(DEV // PB,),
-        in_specs=[
-            whole((NJ, NK, NLON)),
-            whole((NJ, NK, NLON)),
-            whole((NJ, NLON)),
-            whole((1, 128)),
-            whole((4, 128)),
-            table,
-            table,
+        grid=(4,),
+        in_specs=[hbm, hbm, hbm, whole((1, 128)), whole((4, 128)), table, table],
+        out_specs=whole((DEV * RIN, 128)),
+        out_shape=jax.ShapeDtypeStruct((DEV * RIN, 128), F32),
+        scratch_shapes=[
+            pltpu.VMEM((2, 2, 384, HALF), BF16),
+            pltpu.VMEM((128, NLON), F32),
+            pltpu.VMEM((2, NJ, NK, NLON), F32),
+            pltpu.VMEM((NJ, NLON), jnp.int32),
+            pltpu.VMEM((DEV, 128), F32),
+            pltpu.VMEM((DEV, 128), F32),
+            pltpu.SemaphoreType.DMA((3,)),
         ],
-        out_specs=pl.BlockSpec((PB * RIN, 128), lambda g: (g, 0)),
-        out_shape=jax.ShapeDtypeStruct((DEV * RIN, 128), F32),
-        scratch_shapes=[pltpu.VMEM((2, 2, 384, HALF), BF16), pltpu.VMEM((128, NLON), F32)],
         compiler_params=pltpu.CompilerParams(vmem_limit_bytes=48 << 20),
         name="forward",
     )(u, q, ice, mat, ker, th, tl)
 
 
-def middle_kernel(
-    dev_ref, gain_ref, mu_ref, dec_ref, con_ref, b_ref, ph_ref, pl_ref, wt_ref, o_ref,
-    u_ref, q_ref, s_ref, st_ref, dc_ref, g_ref, r_ref, z_ref, rt_ref,
-):
-    p = dev_ref[0]
-    par = p % 2
+def lane_tables():
     shape = (NI, 128)
     lane = lax.broadcasted_iota(jnp.int32, shape, 1)
     row = lax.broadcasted_iota(jnp.int32, shape, 0)
+    return shape, lane, row
+
+
+def take(x, index):
+    return jnp.take_along_axis(x, index, axis=1)
+
+
+def load_materials(b_ref, mu_ref, dec_ref, con_ref, s_ref, st_ref, dc_ref, g_ref, r_ref):
+    shape, lane, row = lane_tables()
     r = lane & 3
-    j = (lane >> 2) & 15
-    first = lane < 64
-    rp = (lane & ~3) | ((lane + 1) & 3)
-    rm = (lane & ~3) | ((lane + 3) & 3)
-    jp = (lane & 64) | ((lane + 4) & 63)
-    jm = (lane & 64) | ((lane + 60) & 63)
-
-    def take(x, index):
-        return jnp.take_along_axis(x, index, axis=1)
-
-    zero = jnp.zeros(shape, F32)
-    for buf in range(2):
-        for kk in range(2):
-            u_ref[buf, kk, 0] = zero
-            u_ref[buf, kk, NB + 1] = zero
     for b in range(NB):
         extra = b_ref[pl.ds(b * RIN + 4, NI, stride=NB * RIN), :]
         mat = take(extra, 64 + (lane & 63))
@@ -189,17 +201,32 @@
         stiff = look(mu_ref)
         st_ref[b] = stiff
         dc_ref[b] = look(dec_ref)
-        r_ref[b] = look(con_ref)
+        if r_ref is not None:
+            r_ref[b] = look(con_ref)
         g_ref[b] = (RELAX / DIAG) / stiff
         layer = (r + (4 * b + 1)).astype(F32) * (LOAD / NR)
         for kk in range(2):
             s_ref[kk, b] = take(extra, kk * 32 + (lane >> 2)) * layer
-            u_ref[0, kk, b + 1] = b_ref[pl.ds(b * RIN + kk, NI, stride=NB * RIN), :]
-            q_ref[kk, b] = b_ref[pl.ds(b * RIN + 2 + kk, NI, stride=NB * RIN), :]
-
-    gains = [jnp.where(first, gain_ref[4 * p + 2 * kk], gain_ref[4 * p + 2 * kk + 1]) for kk in range(2)]
-
-    def sweep(src, dst):
+
+
+def three_sweeps(p, gain_ref, u_ref, q_ref, s_ref, st_ref, dc_ref, g_ref):
+    shape, lane, row = lane_tables()
+    r = lane & 3
+    j = (lane >> 2) & 15
+    rp = (lane & ~3) | ((lane + 1) & 3)
+    rm = (lane & ~3) | ((lane + 3) & 3)
+    jp = (lane & 64) | ((lane + 4) & 63)
+    jm = (lane & 64) | ((lane + 60) & 63)
+    gains = [jnp.where(lane < 64, gain_ref[4 * p + 2 * kk], gain_ref[4 * p + 2 * kk + 1]) for kk in range(2)]
+    zero = jnp.zeros(shape, F32)
+    for buf in range(2):
+        for kk in range(2):
+            u_ref[buf, kk, 0] = zero
+            u_ref[buf, kk, NB + 1] = zero
+
+    def body(step, carry):
+        src = step % 2
+        dst = 1 - src
         for kk in range(2):
             for b in range(NB):
                 uc = u_ref[src, kk, b + 1]
@@ -213,16 +240,31 @@
                 un = gains[kk] * uc + g_ref[b] * (s_ref[kk, b] - q) + (RELAX / DIAG) * beside
                 u_ref[dst, kk, b + 1] = un
                 q_ref[kk, b] = dc_ref[b] * q + st_ref[b] * (un - uc)
-
-    def three(start):
-        def body(step, carry):
-            src = (start + step) % 2
-            sweep(src, 1 - src)
-            return carry
-
-        lax.fori_loop(0, 3, body, 0)
-
-    three(0)
+        return carry
+
+    lax.fori_loop(0, 3, body, 0)
+
+
+def half_kernel(b_ref, o_ref):
+    for t in range(2):
+        o_ref[pl.ds(t * DEV, DEV), :] = b_ref[pl.ds(5 + t, DEV, stride=RIN), :]
+
+
+def first_kernel(
+    dev_ref, gain_ref, mu_ref, dec_ref, con_ref, b_ref, ph_ref, pl_ref, wt_ref, u3_ref, q_ref, c_ref,
+    u_ref, s_ref, st_ref, dc_ref, g_ref, r_ref, z_ref, rt_ref,
+):
+    p = dev_ref[0]
+    par = p % 2
+    load_materials(b_ref, mu_ref, dec_ref, con_ref, s_ref, st_ref, dc_ref, g_ref, r_ref)
+    for b in range(NB):
+        for kk in range(2):
+            u_ref[0, kk, b + 1] = b_ref[pl.ds(b * RIN + kk, NI, stride=NB * RIN), :]
+            q_ref[kk, b] = b_ref[pl.ds(b * RIN + 2 + kk, NI, stride=NB * RIN), :]
+    three_sweeps(p, gain_ref, u_ref, q_ref, s_ref, st_ref, dc_ref, g_ref)
+    for b in range(NB):
+        for kk in range(2):
+            u3_ref[kk, b] = u_ref[1, kk, b + 1]
     for h in range(NB // 2):
         pair = [r_ref[2 * h + t] * u_ref[1, 0, 2 * h + t + 1] for t in range(2)]
         rt_ref[:, 128 * h : 128 * h + 128] = jnp.concatenate(pair, axis=0).T
@@ -237,15 +279,37 @@
     z4 = jnp.concatenate([z, z, z, z], axis=0)
     zh, zl = split(z4)
     ph, plo = ph_ref[...], pl_ref[...]
-    coef = dot_nt(ph, zh) + (dot_nt(ph, zl) + dot_nt(plo, zh))
+    c_ref[...] = dot_nt(ph, zh) + (dot_nt(ph, zl) + dot_nt(plo, zh))
+
+
+def second_kernel(
+    dev_ref, gain_ref, mu_ref, dec_ref, con_ref, b_ref, ph_ref, pl_ref, u3_ref, q3_ref, c_ref, k_ref, o_ref,
+    u_ref, q_ref, s_ref, st_ref, dc_ref, g_ref, rt_ref, phi_ref,
+):
+    p = dev_ref[0]
+    par = p % 2
+    core = (p // NB) % 2
+    mine = pl.multiple_of(128 * core, 128)
+    other = pl.multiple_of(128 - 128 * core, 128)
+    load_materials(b_ref, mu_ref, dec_ref, con_ref, s_ref, st_ref, dc_ref, g_ref, None)
+    for b in range(NB):
+        for kk in range(2):
+            u_ref[0, kk, b + 1] = u3_ref[kk, b]
+            q_ref[kk, b] = q3_ref[kk, b]
     lane1 = lax.broadcasted_iota(jnp.int32, (128, 128), 1)
     sub1 = lax.broadcasted_iota(jnp.int32, (128, 128), 0)
     phi = jnp.zeros((NDEG, 128), F32)
+    coef_mine = c_ref[pl.ds(mine, 128), :]
+    coef_other = c_ref[pl.ds(other, 128), :]
     for b in range(NB):
         prod = jnp.concatenate(
             [
-                b_ref[pl.ds(b * RIN + 5 + nn, NI, stride=NB * RIN), :] * coef[64 * nn : 64 * nn + 64]
-                for nn in range(4)
+                b_ref[pl.ds(b * RIN + 5 + t, NI, stride=NB * RIN), :] * coef_mine[64 * t : 64 * t + 64]
+                for t in range(2)
+            ]
+            + [
+                k_ref[pl.ds(t * DEV + b, NI, stride=NB), :] * coef_other[64 * t : 64 * t + 64]
+                for t in range(2)
             ],
             axis=0,
         )
@@ -253,15 +317,16 @@
         hi, lo = split(prod)
         phi = phi + (dot_nn(hi, pick) + dot_nn(lo, pick))
     factor = jnp.where(p == 0, 2.0, jnp.where(p == MODES, 0.0, 1.0))
-    phi_t = (phi * factor).T[0:NR]
-    fh, fl = split(phi_t)
+    phi_ref[pl.ds(mine, 128), :] = phi[:128] * factor
+    phi_ref[pl.ds(other, 128), :] = phi[128:] * factor
+    fh, fl = split(phi_ref[...].T[0:NR])
+    ph, plo = ph_ref[...], pl_ref[...]
     pot = dot_nn(fh, ph) + (dot_nn(fl, ph) + dot_nn(fh, plo))
     rt_ref[...] = jnp.zeros(rt_ref.shape, F32)
+    kept_ref = rt_ref.at[pl.ds(pl.multiple_of(64 * par, 64), 64), :]
     for jj in range(NJ):
         for b in range(NB):
-            z_ref2 = pot[4 * b : 4 * b + 4, 64 * jj : 64 * jj + 64]
-            kept_ref = rt_ref.at[pl.ds(pl.multiple_of(64 * par, 64), 64), :]
-            kept_ref[4 * jj : 4 * jj + 4, 64 * b : 64 * b + 64] = z_ref2
+            kept_ref[4 * jj : 4 * jj + 4, 64 * b : 64 * b + 64] = pot[4 * b : 4 * b + 4, 64 * jj : 64 * jj + 64]
     for h in range(NB // 2):
         back = rt_ref[:, 128 * h : 128 * h + 128].T
         for t in range(2):
@@ -269,36 +334,28 @@
             piece = back[64 * t : 64 * t + 64]
             o_ref[pl.ds(b * ROUT + 4, NI, stride=NB * ROUT), :] = piece
             s_ref[0, b] = s_ref[0, b] + COUPLE * piece
-    three(1)
-    for b in range(NB):
-        for kk in range(2):
-            o_ref[pl.ds(b * ROUT + kk, NI, stride=NB * ROUT), :] = u_ref[0, kk, b + 1]
+    three_sweeps(p, gain_ref, u_ref, q_ref, s_ref, st_ref, dc_ref, g_ref)
+    for b in range(NB):
+        for kk in range(2):
+            o_ref[pl.ds(b * ROUT + kk, NI, stride=NB * ROUT), :] = u_ref[1, kk, b + 1]
             o_ref[pl.ds(b * ROUT + 2 + kk, NI, stride=NB * ROUT), :] = q_ref[kk, b]
 
 
-def middle(dev, gain, mu, dec, con, b, ph, plo, wt):
+FIELD = (NB, NI, 128)
+
+
+def local_call(kernel, name, scalars, arrays, out_shape, scratch):
     smem = pl.BlockSpec(memory_space=pltpu.SMEM)
     vmem = pl.BlockSpec(memory_space=pltpu.VMEM)
-    field = (NB, NI, 128)
     return pl.pallas_call(
-        middle_kernel,
-        in_specs=[smem] * 5 + [vmem] * 4,
-        out_specs=vmem,
-        out_shape=jax.ShapeDtypeStruct((DEV * ROUT, 128), F32),
-        scratch_shapes=[
-            pltpu.VMEM((2, 2, NB + 2, NI, 128), F32),
-            pltpu.VMEM((2, *field), F32),
-            pltpu.VMEM((2, *field), F32),
-            pltpu.VMEM(field, F32),
-            pltpu.VMEM(field, F32),
-            pltpu.VMEM(field, F32),
-            pltpu.VMEM(field, F32),
-            pltpu.VMEM((NR, NLAT), F32),
-            pltpu.VMEM((128, DEV), F32),
-        ],
+        kernel,
+        in_specs=[smem] * len(scalars) + [vmem] * len(arrays),
+        out_specs=jax.tree.map(lambda _: vmem, out_shape),
+        out_shape=out_shape,
+        scratch_shapes=[pltpu.VMEM(shape, F32) for shape in scratch],
         compiler_params=pltpu.CompilerParams(vmem_limit_bytes=48 << 20),
-        name="middle",
-    )(dev, gain, mu, dec, con, b, ph, plo, wt)
+        name=name,
+    )(*scalars, *arrays)
 
 
 LB = 256
@@ -371,9 +428,23 @@
         dev = lax.axis_index(ALL).reshape(1)
         packed = forward(displacement, memory, ice_class, mat, ker, th, tl)
         arrived = exchange(packed, RIN)
-        moved = middle(
-            dev, jnp.asarray(gain_np), mu_table, decay_table, contrast_table, arrived,
-            jnp.asarray(ph_np), jnp.asarray(pl_np), jnp.asarray(wt_np),
+        half = local_call(half_kernel, "half", (), (arrived,), jax.ShapeDtypeStruct((DEV * 2, 128), F32), [])
+        swapped = lax.ppermute(half, "lat_2", [(0, 1), (1, 0)])
+        scalars = (dev, jnp.asarray(gain_np), mu_table, decay_table, contrast_table)
+        ph, plo = jnp.asarray(ph_np), jnp.asarray(pl_np)
+        u3, q3, coef = local_call(
+            first_kernel, "first", scalars, (arrived, ph, plo, jnp.asarray(wt_np)),
+            [
+                jax.ShapeDtypeStruct((2, *FIELD), F32),
+                jax.ShapeDtypeStruct((2, *FIELD), F32),
+                jax.ShapeDtypeStruct((NDEG, 128), F32),
+            ],
+            [(2, 2, NB + 2, NI, 128), (2, *FIELD), FIELD, FIELD, FIELD, FIELD, (NR, NLAT), (128, DEV)],
+        )
+        moved = local_call(
+            second_kernel, "second", scalars, (arrived, ph, plo, u3, q3, coef, swapped),
+            jax.ShapeDtypeStruct((DEV * ROUT, 128), F32),
+            [(2, 2, NB + 2, NI, 128), (2, *FIELD), (2, *FIELD), FIELD, FIELD, FIELD, (128, DEV), (NDEG, 128)],
         )
         returned = exchange(moved, ROUT)
         return tuple(inverse(returned, th, tl))

time: 166 us -> 154 us (0.928)
  blocking collectives: 47.3 us -> 120 us
  waiting for transfers between devices: 61.2 us -> 0.01 us
  starting transfers between devices: 22.2 us -> 2.09 us
  local copies, waits for them, and re-layouts: 4.06 us -> 1.06 us
    all_to_all x1 -> x2, blocking collectives: 47.3 us -> 120 us  [exchange(): x = lax.all_to_all(x, ALL, split_axis=0, concat_axis=0, tiled=True)]
    all_to_all x1 -> x0, waiting for transfers between devices: 61.2 us -> none  [exchange(): x = lax.all_to_all(x, ALL, split_axis=0, concat_axis=0, tiled=True)]
    all_to_all x1 -> x0, starting transfers between devices: 22.2 us -> none  [exchange(): x = lax.all_to_all(x, ALL, split_axis=0, concat_axis=0, tiled=True)]
    unnamed x22 -> x16, local copies, waits for them, and re-layouts: 3.04 us -> 0.04 us
    ppermute x0 -> x1, starting transfers between devices: none -> 2.09 us  [per_device(): swapped = lax.ppermute(half, 'lat_2', [(0, 1), (1, 0)])]
    pallas_call x2 -> x4, Pallas kernels: 22.8 us -> 21.9 us  [the longest x3 13.6 us: local_call(): pl.pallas_call(kernel, in_specs=[smem] * len(scalars) + [vmem] * len(arra...]
  transfers between devices with their start and end apart: 1 -> 1, of which waited for: 1 -> 0; matrix products, arithmetic and copies ran while one was open for 0% -> 0% of each run, Pallas kernels for 0% -> 4%
where the time goes in v2:
time: 154 us; the launch traced here: 153 us
  blocking collectives  120 us (78%)
  Pallas kernels  28.8 us (19%)
  starting transfers between devices  2.09 us (1%)
    all_to_all x2, blocking collectives, exchange(): x = lax.all_to_all(x, ALL, split_axis=0, concat_axis=0, tiled=True)  120 us
    pallas_call x3, Pallas kernels, local_call(): pl.pallas_call(kernel, in_specs=[smem] * len(scalars) + [vmem] * len(arra...  13.6 us
    pallas_call x1, Pallas kernels, forward(): pl.pallas_call(forward_kernel, grid=(4,), in_specs=[hbm, hbm, hbm, whole(...  8.39 us
    pallas_call x1, Pallas kernels, inverse(): pl.pallas_call(inverse_kernel, grid=(HALF // LB,), in_specs=[whole((DEV *...  6.84 us
  transfers between devices with their start and end apart: 1, of which 0 were waited for; matrix products, arithmetic and copies ran while one was open for 0% of the time, Pallas kernels for 4%

profile of v2, /device:TPU:1, one launch (start us, length us, event | category | flops | bytes accessed | tf_op | source)
XLA Modules:
  0.0 153.3 jit_solution(7816765757857152567)
XLA Ops:
  0.6 0.7 convert_element_type.16
  1.3 0.8 reshape.43.ker_ref
  2.1 0.1 copy.19
  2.2 0.1 convert_element_type.17
  2.3 0.1 pad.4.mat_ref
  2.3 8.4 %forward.1 = f32[3584,128]{1,0:T(8,128)S(1)} custom-call(f32[16,4,2048]{2,1,0:T(4,128)} %u_hbm.1, f32[16,4,2048]{2,1,0:T(4,128)} %q_hbm.1, s32[16,2048]{1,0:T(8,128)} %ice_hbm.1, f32[1,128]{1,0:T(1,128)S(1)} %pad.4.mat_ref, f32[4,128]{1,0:T(4,128)S(1)} %reshape.43.ker_ref, bf16[2,2,512,1024]{3,2,1,0:T(8,128)(2,1)} %constant.42.clone.th_ref, ...), custom_call_target="tpu_custom_call" | custom-call | tf_op jit(solution)/shard_map/forward/pallas_call | solution.py:157
  10.7 72.0 %all_to_all.18 = f32[512,1,896]{2,1,0:T(1,128)S(1)} all-to-all(f32[512,1,896]{2,1,0:T(1,128)S(1)} %bitcast.8), channel_id=1, replica_groups=mesh['lat_0'=4,'lat_1'=8,'lat_2'=2,'rad_0'=4,'rad_1'=2] {'lat_0','lat_1'..., dimensions={0} | all-to-all | bytes 3670016 | tf_op jit(solution)/shard_map/all_to_all | solution.py:413
  82.7 0.0 copy-start.1
  82.7 0.0 copy-start.2
  82.7 0.0 copy-start.3
  82.7 0.0 copy-start.4
  82.7 0.0 copy-start.5
  82.7 0.0 copy-start.6
  82.7 0.0 copy-start.7
  82.8 2.1 %collective-permute-start = (f32[1024,128]{1,0:T(8,128)S(1)}, f32[1024,128]{1,0:T(8,128)}, u32[]{:S(2)}, u32[]{:S(2)}) collective-permute-start(f32[1024,128]{1,0:T(8,128)S(1)} %half.1), channel_id=1, source_target_pairs={{0,8},{8,0},{1,9},{9,1},{2,10},{10,2},{3,11},{11,3},{4,12},{12,4},... | collective-permute-start | bytes 1572872 | tf_op jit(solution)/shard_map/ppermute | solution.py:432
  84.9 0.0 copy-done.1
  84.9 0.0 copy-done.2
  84.9 0.0 copy-done.3
  84.9 0.0 copy-done.4
  84.9 0.0 copy-done.5
  85.0 0.0 copy-done.6
  85.0 0.0 copy-done.7
  85.0 6.5 %first.1 = (f32[2,8,64,128]{3,2,1,0:T(8,128)S(1)}, f32[2,8,64,128]{3,2,1,0:T(8,128)S(1)}, f32[256,128]{1,0:T(8,128)S(1)}) custom-call(s32[1]{0:T(128)} %bitcast.dev_ref, f32[2048]{0:T(1024)S(1)} %copy-done.3, f32[8]{0:T(128)S(1)} %copy-done.5, f32[8]{0:T(128)S(1)} %copy-done.6, f32[8]{0:T(128)S(1)} %copy-done.7, f32[3584,128]{1,0:T(8,128)S(1)} %bitcast.6, ...), custom_call_target="tpu_custom_call" | custom-call | tf_op jit(solution)/shard_map/first/pallas_call | solution.py:350
  91.4 0.0 collective-permute-done.k_ref
  91.5 0.0 copy-start
  91.5 7.1 %second.1 = f32[2560,128]{1,0:T(8,128)S(1)} custom-call(s32[1]{0:T(128)} %bitcast.dev_ref, f32[2048]{0:T(1024)S(1)} %copy-done.3, f32[8]{0:T(128)S(1)} %copy-done.5, f32[8]{0:T(128)S(1)} %copy-done.6, f32[8]{0:T(128)S(1)} %copy-done.7, f32[3584,128]{1,0:T(8,128)S(1)} %bitcast.7, bf16[256,1024]{1,0:T(8,128)(2,1)S(1)} %copy-done.2, ...), custom_call_target="tpu_custom_call" | custom-call | tf_op jit(solution)/shard_map/second/pallas_call | solution.py:350
  98.5 47.9 %all_to_all.19 = f32[512,1,640]{2,1,0:T(1,128)S(1)} all-to-all(f32[512,1,640]{2,1,0:T(1,128)S(1)} %bitcast.10), channel_id=1, replica_groups=mesh['lat_0'=4,'lat_1'=8,'lat_2'=2,'rad_0'=4,'rad_1'=2] {'lat_0','lat_1'..., dimensions={0} | all-to-all | bytes 2621440 | tf_op jit(solution)/shard_map/all_to_all | solution.py:413
  146.5 0.0 copy-done
  146.5 6.8 %inverse.1 = (f32[16,4,2048]{2,1,0:T(4,128)}, f32[16,4,2048]{2,1,0:T(4,128)}, f32[16,4,2048]{2,1,0:T(4,128)}) custom-call(f32[2560,128]{1,0:T(8,128)S(1)} %bitcast.9, bf16[2,2,512,1024]{3,2,1,0:T(8,128)(2,1)S(1)} %copy-done, bf16[2,2,512,1024]{3,2,1,0:T(8,128)(2,1)} %constant.43.clone.tl_ref), custom_call_target="tpu_custom_call" | custom-call | tf_op jit(solution)/shard_map/inverse/pallas_call | solution.py:399
  (1 shorter events, 0.0 us)
Async XLA Ops:
  82.7 2.2 %copy-start.1 = (bf16[256,1024]{1,0:T(8,128)(2,1)S(1)}, bf16[256,1024]{1,0:T(8,128)(2,1)}, u32[]{:S(2)}) copy-start(bf16[256,1024]{1,0:T(8,128)(2,1)} %constant.46.clone.pl_ref) | copy-start | bytes 1572868
  82.7 2.2 %copy-start.2 = (bf16[256,1024]{1,0:T(8,128)(2,1)S(1)}, bf16[256,1024]{1,0:T(8,128)(2,1)}, u32[]{:S(2)}) copy-start(bf16[256,1024]{1,0:T(8,128)(2,1)} %constant.45.clone.ph_ref) | copy-start | bytes 1572868
  82.7 2.2 %copy-start.3 = (f32[2048]{0:T(1024)S(1)}, f32[2048]{0:T(1024)}, u32[]{:S(2)}) copy-start(f32[2048]{0:T(1024)} %constant.44.clone.gain_ref) | copy-start | bytes 24580
  82.7 2.2 %copy-start.4 = (f32[1,1024]{1,0:T(1,128)S(1)}, f32[1,1024]{1,0:T(1,128)}, u32[]{:S(2)}) copy-start(f32[1,1024]{1,0:T(1,128)} %constant.47.clone.wt_ref) | copy-start | bytes 12292
  82.7 2.2 %copy-start.5 = (f32[8]{0:T(128)S(1)}, f32[8]{0:T(128)}, u32[]{:S(2)}) copy-start(f32[8]{0:T(128)} %mu_ref.3) | copy-start | bytes 100
  82.7 2.2 %copy-start.6 = (f32[8]{0:T(128)S(1)}, f32[8]{0:T(128)}, u32[]{:S(2)}) copy-start(f32[8]{0:T(128)} %dec_ref.3) | copy-start | bytes 100
  82.7 2.2 %copy-start.7 = (f32[8]{0:T(128)S(1)}, f32[8]{0:T(128)}, u32[]{:S(2)}) copy-start(f32[8]{0:T(128)} %con_ref.3) | copy-start | bytes 100
  82.8 8.7 %collective-permute-start = (f32[1024,128]{1,0:T(8,128)S(1)}, f32[1024,128]{1,0:T(8,128)}, u32[]{:S(2)}, u32[]{:S(2)}) collective-permute-start(f32[1024,128]{1,0:T(8,128)S(1)} %half.1), channel_id=1, source_target_pairs={{0,8},{8,0},{1,9},{9,1},{2,10},{10,2},{3,11},{11,3},{4,12},{12,4},... | collective-permute-start | bytes 1572872 | tf_op jit(solution)/shard_map/ppermute | solution.py:432
  91.5 55.0 %copy-start = (bf16[2,2,512,1024]{3,2,1,0:T(8,128)(2,1)S(1)}, bf16[2,2,512,1024]{3,2,1,0:T(8,128)(2,1)}, u32[]{:S(2)}) copy-start(bf16[2,2,512,1024]{3,2,1,0:T(8,128)(2,1)} %constant.42.clone.th_ref) | copy-start | bytes 12582916

commit v3 on v2

--- a/solution.py
+++ b/solution.py
@@ -27,35 +27,33 @@
     return hi, lo
 
 
-def order_tables():
-    kind = np.zeros((2, 2, DEV), np.int64)
-    order = np.zeros((2, 2, DEV), np.int64)
+def fourier_tables():
+    kind = np.zeros((2, DEV), np.int64)
+    order = np.zeros((2, DEV), np.int64)
     for par in range(2):
-        high = [(k, c) for c in range(MODES + par, HALF, 2) for k in (0, 1)]
-        rest = iter(high)
-        for kk in range(2):
-            for p in range(DEV):
-                if kk == 0 and p % 2 == par:
-                    k, c = (0, p) if p < MODES else (1, p - MODES)
-                    if k == 1 and c == 0:
-                        k, c = 0, HALF
-                else:
-                    k, c = next(rest)
-                kind[par, kk, p], order[par, kk, p] = k, c
-    return kind, order
-
-
-def fourier_tables():
-    kind, order = order_tables()
+        rest = iter([(k, c) for c in range(MODES + par, 2 * MODES, 2) for k in (0, 1)])
+        for p in range(DEV):
+            if p % 2 == par:
+                k, c = (0, p) if p < MODES else (1, p - MODES)
+            else:
+                k, c = next(rest)
+            kind[par, p], order[par, p] = k, c
+    order[0, MODES] = HALF // 2
     l = np.arange(HALF)
-    phase = (order[..., None] * l) % NLON
-    angle = phase * (2.0 * np.pi / NLON)
-    value = np.where(kind[..., None] == 0, np.cos(angle), np.sin(angle)) * np.sqrt(2.0 / NLON)
-    value = np.where((order % HALF == 0)[..., None], value * np.sqrt(0.5), value)
+    angle = (order[..., None] * l) % NLON * (2.0 * np.pi / NLON)
+    cos, sin = np.cos(angle), np.sin(angle)
+    value = np.where(kind[..., None] == 0, cos, sin) * np.sqrt(2.0 / NLON)
+    value[0, 0] = np.sqrt(1.0 / NLON)
+    value[0, MODES] = (cos[0, MODES] + sin[0, MODES]) * np.sqrt(1.0 / NLON)
+    block, t = np.arange(HALF // 2) // 128, np.arange(HALF // 2) % 128
+    even = 256 * block + np.where(t % 2 == 0, t, 128 + t - 1)
+    odd = 256 * block + np.where(t % 2 == 0, t + 1, 128 + t)
+    value = np.stack([value[..., even], value[..., odd]], axis=1)
     eigen = 2.0 * np.cos(order * (2.0 * np.pi / NLON))
+    eigen = np.stack([eigen, -eigen])
     gain = (1.0 - RELAX) + RELAX / DIAG * eigen
     hi, lo = split_np(value)
-    return hi, lo, np.ascontiguousarray(gain.transpose(2, 1, 0).reshape(DEV * 4)).astype(np.float32)
+    return hi, lo, np.ascontiguousarray(gain.transpose(2, 0, 1).reshape(DEV * 4)).astype(np.float32)
 
 
 def legendre_tables():
@@ -87,91 +85,106 @@
     return lax.dot_general(a, b, (((1,), (0,)), ((), ())), preferred_element_type=F32)
 
 
+QUART = HALF // 2
+
+
 def forward_kernel(
-    u_hbm, q_hbm, ice_hbm, mat_ref, ker_ref, th_ref, tl_ref, a_ref, x_ref, w_ref, f_ref, ice_ref, even_ref, extra_ref, sem
+    u_hbm, q_hbm, ice_hbm, th_hbm, tl_hbm, mat_ref, ker_ref, a_ref, x_ref, w_ref, f_ref, ice_ref, th_ref, tl_ref, sem
 ):
-    g = pl.program_id(0)
-    kk, k2 = g // 2, g % 2
-
-    @pl.when(g == 0)
-    def _():
-        copies = [
-            pltpu.make_async_copy(u_hbm, f_ref.at[0], sem.at[0]),
-            pltpu.make_async_copy(q_hbm, f_ref.at[1], sem.at[1]),
-            pltpu.make_async_copy(ice_hbm, ice_ref, sem.at[2]),
-        ]
-        for copy in copies:
-            copy.start()
-        x_ref[:, :, 256:, :] = jnp.zeros((2, 2, 128, HALF), BF16)
-        peer = lax.broadcasted_iota(jnp.int32, (DEV, 128), 0)
-        core = (peer >> 3) & 1
+    copies = [
+        pltpu.make_async_copy(u_hbm, f_ref.at[0], sem.at[0]),
+        pltpu.make_async_copy(q_hbm, f_ref.at[1], sem.at[1]),
+        pltpu.make_async_copy(ice_hbm, ice_ref, sem.at[2]),
+    ]
+    for k2 in range(2):
+        for e in range(2):
+            n = 3 + 4 * k2 + 2 * e
+            copies.append(pltpu.make_async_copy(th_hbm.at[k2, e], th_ref.at[k2, e], sem.at[n]))
+            copies.append(pltpu.make_async_copy(tl_hbm.at[k2, e], tl_ref.at[k2, e], sem.at[n + 1]))
+    for copy in copies:
+        copy.start()
+    peer = lax.broadcasted_iota(jnp.int32, (DEV, 128), 0)
+    lane = lax.broadcasted_iota(jnp.int32, (DEV, 128), 1)
+    core = (peer >> 3) & 1
+    ker = jnp.concatenate([ker_ref[:, rr, :] for rr in range(NK)], axis=1)
+    for t in range(2):
+        a_ref[pl.ds(5 + t, DEV, stride=RIN), :] = jnp.where(core == 0, ker[t : t + 1], ker[2 + t : 3 + t])
+    place = lax.broadcasted_iota(jnp.int32, (NJ, 128), 0)
+    column = lax.broadcasted_iota(jnp.int32, (NJ, 128), 1)
+    spread = ((column >> 2) == place + NJ).astype(BF16)
+    mat = dot_nn(mat_ref[...].astype(F32).astype(BF16), spread)
+    mat = jnp.where((lane[:NK] & 3) == peer[:NK], mat, 0.0)
+    extra = jnp.broadcast_to(jnp.sum(mat, axis=0, keepdims=True), (DEV, 128))
+    x_ref[:, :, 256:, :] = jnp.zeros((2, 2, 128, QUART), BF16)
+    for f in range(2):
+        copies[f].wait()
+        for j in range(NJ):
+            w_ref[pl.ds(64 * f + 4 * j, 4), :] = f_ref[f, j]
+    copies[2].wait()
+    w_ref[pl.ds(128, NJ), :] = ice_ref[...].astype(F32)
+    rows = 128 + NJ
+    parity = lax.broadcasted_iota(jnp.int32, (rows, 128), 1) & 1
+    for m in range(HALF // 256):
+        parts = []
         for t in range(2):
-            mine = jnp.where(core == 0, ker_ref[pl.ds(t, 1), :], ker_ref[pl.ds(2 + t, 1), :])
-            a_ref[pl.ds(5 + t, DEV, stride=RIN), :] = mine
-        for f in range(2):
-            copies[f].wait()
-            for j in range(NJ):
-                w_ref[pl.ds(64 * f + 4 * j, 4), :] = f_ref[f, j]
-        copies[2].wait()
-        low, high = w_ref[:, :HALF], w_ref[:, HALF:]
-        ice = ice_ref[...].astype(F32)
-        il, ih = ice[:, :HALF], ice[:, HALF:]
-        for par in range(2):
-            part = low + high if par == 0 else low - high
-            ipart = il + ih if par == 0 else il - ih
-            ph, plo = split(part)
-            for slot in range(2):
-                x_ref[slot, par, 0:128, :] = plo
-                x_ref[slot, par, 128:256, :] = ph
-                x_ref[slot, par, pl.ds(256 + (slot * 2 + par) * NJ, NJ), :] = ipart.astype(BF16)
-        extra_ref[...] = jnp.broadcast_to(mat_ref[...], (DEV, 128))
-
-    first = lax.broadcasted_iota(jnp.int32, (DEV, 128), 1) < 64
-    x = x_ref[kk, k2]
-    r1 = dot_nt(th_ref[0, 0], x)
-    r2 = dot_nt(tl_ref[0, 0], x[128:])
-    main = r1[:, 128:256] + (r1[:, :128] + r2[:, :128])
-    extra_ref[...] += r1[:, 256:] + r2[:, 128:]
-
-    @pl.when(k2 == 0)
-    def _():
-        even_ref[...] = main
-
-    @pl.when(k2 == 1)
-    def _():
-        even = even_ref[...]
-        a_ref[pl.ds(kk, DEV, stride=RIN), :] = jnp.where(first, even, pltpu.roll(main, 64, 1))
-        a_ref[pl.ds(2 + kk, DEV, stride=RIN), :] = jnp.where(first, pltpu.roll(even, 64, 1), main)
-
-    @pl.when(g == 3)
-    def _():
-        a_ref[pl.ds(4, DEV, stride=RIN), :] = extra_ref[...]
+            start = 256 * m + 128 * t
+            low, high = w_ref[:, start : start + 128], w_ref[:, HALF + start : HALF + start + 128]
+            parts.append((low + high, low - high))
+        for k2 in range(2):
+            v0, v1 = parts[0][k2], parts[1][k2]
+            for e, value in (
+                (0, jnp.where(parity == 0, v0, pltpu.roll(v1, 1, 1))),
+                (1, jnp.where(parity == 0, pltpu.roll(v0, 127, 1), v1)),
+            ):
+                hi, lo = split(value[:128])
+                cols = slice(128 * m, 128 * m + 128)
+                x_ref[k2, e, 0:128, cols] = lo
+                x_ref[k2, e, 128:256, cols] = hi
+                x_ref[k2, e, 256 + NJ * k2 : 256 + NJ * k2 + NJ, cols] = value[128:].astype(BF16)
+    first = lane < 64
+    slots = []
+    ice_sum = [0.0, 0.0]
+    for k2 in range(2):
+        product = []
+        for e in range(2):
+            n = 3 + 4 * k2 + 2 * e
+            copies[n].wait()
+            copies[n + 1].wait()
+            x = x_ref[k2, e]
+            r1 = dot_nt(th_ref[k2, e], x)
+            r2 = dot_nt(tl_ref[k2, e], x[128:])
+            product.append(r1[:, 128:256] + (r1[:, :128] + r2[:, :128]))
+            ice_sum[e] = ice_sum[e] + (r1[:, 256:] + r2[:, 128:])
+        slots.append((product[0] + product[1], product[0] - product[1]))
+    for kk in range(2):
+        even, odd = slots[0][kk], slots[1][kk]
+        a_ref[pl.ds(kk, DEV, stride=RIN), :] = jnp.where(first, even, pltpu.roll(odd, 64, 1))
+        a_ref[pl.ds(2 + kk, DEV, stride=RIN), :] = jnp.where(first, pltpu.roll(even, 64, 1), odd)
+    extra = extra + (ice_sum[0] + ice_sum[1]) + pltpu.roll(ice_sum[0] - ice_sum[1], 32, 1)
+    a_ref[pl.ds(4, DEV, stride=RIN), :] = extra
 
 
 def forward(u, q, ice, mat, ker, th, tl):
-    whole = lambda shape: pl.BlockSpec(shape, lambda g: (0,) * len(shape))
     hbm = pl.BlockSpec(memory_space=pltpu.MemorySpace.HBM)
-    u, q, ice = (pltpu.with_memory_space_constraint(x, pltpu.MemorySpace.HBM) for x in (u, q, ice))
-    th, tl = (pltpu.with_memory_space_constraint(x, pltpu.MemorySpace.HBM) for x in (th, tl))
-    table = pl.BlockSpec((1, 1, DEV, HALF), lambda g: (g % 2, g // 2, 0, 0))
+    vmem = pl.BlockSpec(memory_space=pltpu.VMEM)
+    far = [pltpu.with_memory_space_constraint(x, pltpu.MemorySpace.HBM) for x in (u, q, ice, th, tl)]
     return pl.pallas_call(
         forward_kernel,
-        grid=(4,),
-        in_specs=[hbm, hbm, hbm, whole((1, 128)), whole((4, 128)), table, table],
-        out_specs=whole((DEV * RIN, 128)),
+        in_specs=[hbm] * 5 + [vmem] * 2,
+        out_specs=vmem,
         out_shape=jax.ShapeDtypeStruct((DEV * RIN, 128), F32),
         scratch_shapes=[
-            pltpu.VMEM((2, 2, 384, HALF), BF16),
-            pltpu.VMEM((128, NLON), F32),
+            pltpu.VMEM((2, 2, 384, QUART), BF16),
+            pltpu.VMEM((128 + NJ, NLON), F32),
             pltpu.VMEM((2, NJ, NK, NLON), F32),
             pltpu.VMEM((NJ, NLON), jnp.int32),
-            pltpu.VMEM((DEV, 128), F32),
-            pltpu.VMEM((DEV, 128), F32),
-            pltpu.SemaphoreType.DMA((3,)),
+            pltpu.VMEM((2, 2, DEV, QUART), BF16),
+            pltpu.VMEM((2, 2, DEV, QUART), BF16),
+            pltpu.SemaphoreType.DMA((11,)),
         ],
         compiler_params=pltpu.CompilerParams(vmem_limit_bytes=48 << 20),
         name="forward",
-    )(u, q, ice, mat, ker, th, tl)
+    )(*far, mat, ker)
 
 
 def lane_tables():
@@ -224,9 +237,8 @@
             u_ref[buf, kk, 0] = zero
             u_ref[buf, kk, NB + 1] = zero
 
-    def body(step, carry):
-        src = step % 2
-        dst = 1 - src
+    for step in range(3):
+        src, dst = step % 2, 1 - step % 2
         for kk in range(2):
             for b in range(NB):
                 uc = u_ref[src, kk, b + 1]
@@ -240,9 +252,6 @@
                 un = gains[kk] * uc + g_ref[b] * (s_ref[kk, b] - q) + (RELAX / DIAG) * beside
                 u_ref[dst, kk, b + 1] = un
                 q_ref[kk, b] = dc_ref[b] * q + st_ref[b] * (un - uc)
-        return carry
-
-    lax.fori_loop(0, 3, body, 0)
 
 
 def half_kernel(b_ref, o_ref):
@@ -358,51 +367,70 @@
     )(*scalars, *arrays)
 
 
-LB = 256
-
-
-def inverse_kernel(b_ref, th_ref, tl_ref, u_ref, q_ref, p_ref, y_ref):
-    @pl.when(pl.program_id(0) == 0)
-    def _():
-        for f in range(3):
-            for kk in range(2):
-                if f == 2 and kk == 1:
-                    continue
-                rows = b_ref[pl.ds(4 if f == 2 else 2 * f + kk, DEV, stride=ROUT), :].T
-                hi, lo = split(rows)
-                for k2 in range(2):
-                    y_ref[k2, 64 * f : 64 * f + 64, DEV * kk : DEV * kk + DEV] = hi[64 * k2 : 64 * k2 + 64]
-                    y_ref[k2, 192 + 64 * f : 256 + 64 * f, DEV * kk : DEV * kk + DEV] = lo[64 * k2 : 64 * k2 + 64]
+def inverse_kernel(b_ref, th_ref, tl_ref, u_hbm, q_hbm, p_hbm, y_ref, out_ref, sem):
+    for f in range(3):
+        slot = [b_ref[pl.ds(4 if f == 2 else 2 * f + kk, DEV, stride=ROUT), :] for kk in range(1 if f == 2 else 2)]
+        pair = [slot[0].T] * 2 if f == 2 else [(slot[0] + slot[1]).T, (slot[0] - slot[1]).T]
+        for e in range(2):
+            hi, lo = split(pair[e])
+            for k2 in range(2):
+                y_ref[k2, e, 64 * f : 64 * f + 64, :] = hi[64 * k2 : 64 * k2 + 64]
+                y_ref[k2, e, 192 + 64 * f : 256 + 64 * f, :] = lo[64 * k2 : 64 * k2 + 64]
+    parity = lax.broadcasted_iota(jnp.int32, (192, 128), 1) & 1
+    copies = []
+    for n in range(2):
+        cols = slice(256 * n, 256 * n + 256)
+        halves = []
         for k2 in range(2):
-            for base in (128, 320):
-                y_ref[k2, base : base + 64, DEV:] = jnp.zeros((64, DEV), BF16)
-
-    halves = []
-    for k2 in range(2):
-        th = th_ref[k2].reshape(2 * DEV, LB)
-        tl = tl_ref[k2].reshape(2 * DEV, LB)
-        y = y_ref[k2]
-        r1 = dot_nn(y, th)
-        halves.append(r1[:192] + (r1[192:] + dot_nn(y[:192], tl)))
-    even, odd = halves
-    start = pl.multiple_of(pl.program_id(0) * LB, LB)
-    for base, value in ((0, even + odd), (HALF, even - odd)):
-        for f, ref in enumerate((u_ref, q_ref, p_ref)):
-            for j in range(NJ):
-                ref[j, :, pl.ds(base + start, LB)] = value[64 * f + 4 * j : 64 * f + 4 * j + 4]
+            made = []
+            for e in range(2):
+                y = y_ref[k2, e]
+                th, tl = th_ref[k2, e, :, cols], tl_ref[k2, e, :, cols]
+                r1 = dot_nn(y, th)
+                made.append(r1[:192] + (r1[192:] + dot_nn(y[:192], tl)))
+            halves.append(made)
+        for t in range(2):
+            m = 2 * n + t
+            both = []
+            for k2 in range(2):
+                even, odd = (x[:, 128 * t : 128 * t + 128] for x in halves[k2])
+                both.append(
+                    (
+                        jnp.where(parity == 0, even, pltpu.roll(odd, 1, 1)),
+                        jnp.where(parity == 0, pltpu.roll(even, 127, 1), odd),
+                    )
+                )
+            for v in range(2):
+                for base, value in ((0, both[0][v] + both[1][v]), (HALF, both[0][v] - both[1][v])):
+                    start = base + 256 * m + 128 * v
+                    for f in range(3):
+                        for j in range(NJ):
+                            row = 64 * f + 4 * j
+                            out_ref[f, j, :, start : start + 128] = value[row : row + 4]
+        for f, ref in enumerate((u_hbm, q_hbm, p_hbm)):
+            for h in range(2):
+                span = pl.ds(HALF * h + 512 * n, 512)
+                copy = pltpu.make_async_copy(out_ref.at[f, :, :, span], ref.at[:, :, span], sem.at[n, f, h])
+                copy.start()
+                copies.append(copy)
+    for copy in copies:
+        copy.wait()
 
 
 def inverse(b, th, tl):
-    whole = lambda shape: pl.BlockSpec(shape, lambda g: (0,) * len(shape))
-    table = pl.BlockSpec((2, 2, DEV, LB), lambda g: (0, 0, 0, g))
+    hbm = pl.BlockSpec(memory_space=pltpu.MemorySpace.HBM)
+    vmem = pl.BlockSpec(memory_space=pltpu.VMEM)
     shape = (NJ, NK, NLON)
     return pl.pallas_call(
         inverse_kernel,
-        grid=(HALF // LB,),
-        in_specs=[whole((DEV * ROUT, 128)), table, table],
-        out_specs=[whole(shape)] * 3,
+        in_specs=[vmem] * 3,
+        out_specs=[hbm] * 3,
         out_shape=[jax.ShapeDtypeStruct(shape, F32)] * 3,
-        scratch_shapes=[pltpu.VMEM((2, 384, HALF), BF16)],
+        scratch_shapes=[
+            pltpu.VMEM((2, 2, 384, DEV), BF16),
+            pltpu.VMEM((3, *shape), F32),
+            pltpu.SemaphoreType.DMA((2, 3, 2)),
+        ],
         compiler_params=pltpu.CompilerParams(vmem_limit_bytes=48 << 20),
         name="inverse",
     )(b, th, tl)
@@ -423,10 +451,8 @@
         displacement, memory, ice_class, material, mu_table, decay_table, contrast_table, gravity_kernel
     ):
         th, tl = jnp.asarray(th_np), jnp.asarray(tl_np)
-        mat = jnp.pad(material.reshape(1, 64).astype(F32), ((0, 0), (64, 0)))
-        ker = gravity_kernel.reshape(4, 128)
         dev = lax.axis_index(ALL).reshape(1)
-        packed = forward(displacement, memory, ice_class, mat, ker, th, tl)
+        packed = forward(displacement, memory, ice_class, material.T, gravity_kernel, th, tl)
         arrived = exchange(packed, RIN)
         half = local_call(half_kernel, "half", (), (arrived,), jax.ShapeDtypeStruct((DEV * 2, 128), F32), [])
         swapped = lax.ppermute(half, "lat_2", [(0, 1), (1, 0)])

time: 154 us -> 141 us (0.916)
  Pallas kernels: 28.8 us -> 16.3 us
    pallas_call x2, Pallas kernels: 15.2 us -> 7.56 us  [the longest x1 4.79 us: forward(): pl.pallas_call(forward_kernel, in_specs=[hbm] * 5 + [vmem] * 2, out_specs...]
    pallas_call x3, Pallas kernels: 13.6 us -> 8.76 us  [local_call(): pl.pallas_call(kernel, in_specs=[smem] * len(scalars) + [vmem] * len(arra...]
  transfers between devices with their start and end apart: 1 -> 1, of which waited for: 0 -> 0; matrix products, arithmetic and copies ran while one was open for 0% -> 0% of each run, Pallas kernels for 4% -> 3%
where the time goes in v3:
time: 141 us
  blocking collectives  120 us (85%)
  Pallas kernels  16.3 us (12%)
  starting transfers between devices  2.27 us (2%)
  local copies, waits for them, and re-layouts  1.42 us (1%)
    all_to_all x2, blocking collectives, exchange(): x = lax.all_to_all(x, ALL, split_axis=0, concat_axis=0, tiled=True)  120 us
    pallas_call x3, Pallas kernels, local_call(): pl.pallas_call(kernel, in_specs=[smem] * len(scalars) + [vmem] * len(arra...  8.76 us
    pallas_call x1, Pallas kernels, forward(): pl.pallas_call(forward_kernel, in_specs=[hbm] * 5 + [vmem] * 2, out_specs...  4.79 us
  transfers between devices with their start and end apart: 1, of which 0 were waited for; matrix products, arithmetic and copies ran while one was open for 0% of the time, Pallas kernels for 3%

profile of v3, /device:TPU:1, one launch (start us, length us, event | category | flops | bytes accessed | tf_op | source)
XLA Modules:
  0.0 141.0 jit_solution(15647659619638255852)
XLA Ops:
  0.6 0.0 copy-start.5
  0.6 0.7 copy-done.5
  1.3 0.0 copy-start.7
  1.3 0.7 copy-done.7
  2.0 4.8 %forward.1 = f32[3584,128]{1,0:T(8,128)S(1)} custom-call(f32[16,4,2048]{2,1,0:T(4,128)} %u_hbm.1, f32[16,4,2048]{2,1,0:T(4,128)} %q_hbm.1, s32[16,2048]{1,0:T(8,128)} %ice_hbm.1, bf16[2,2,512,512]{3,2,1,0:T(8,128)(2,1)} %constant.39.clone.th_hbm.th_ref, bf16[2,2,512,512]{3,2,1,0:T(8,128)(2,1)} %constant.40.clone.tl_hbm.tl_ref, s32[4,16]{1,0:T(4,128)S(1)} %bitcast.12, ...), custom_call_target="tpu_custom_call" | custom-call | tf_op jit(solution)/shard_map/forward/pallas_call | solution.py:171
  6.8 72.0 %all_to_all.18 = f32[512,1,896]{2,1,0:T(1,128)S(1)} all-to-all(f32[512,1,896]{2,1,0:T(1,128)S(1)} %bitcast.9), channel_id=1, replica_groups=mesh['lat_0'=4,'lat_1'=8,'lat_2'=2,'rad_0'=4,'rad_1'=2] {'lat_0','lat_1'..., dimensions={0} | all-to-all | bytes 3670016 | tf_op jit(solution)/shard_map/all_to_all | solution.py:441
  78.8 0.0 copy-start.2
  78.8 0.0 copy-start.3
  78.8 0.0 copy-start.4
  78.8 0.0 copy-start.6
  78.8 0.0 copy-start.8
  78.8 0.0 copy-start.9
  78.8 0.0 copy-start.10
  78.9 2.3 %collective-permute-start = (f32[1024,128]{1,0:T(8,128)S(1)}, f32[1024,128]{1,0:T(8,128)}, u32[]{:S(2)}, u32[]{:S(2)}) collective-permute-start(f32[1024,128]{1,0:T(8,128)S(1)} %half.1), channel_id=1, source_target_pairs={{0,8},{8,0},{1,9},{9,1},{2,10},{10,2},{3,11},{11,3},{4,12},{12,4},... | collective-permute-start | bytes 1572872 | tf_op jit(solution)/shard_map/ppermute | solution.py:458
  81.2 0.0 copy-done.2
  81.2 0.0 copy-done.3
  81.2 0.0 copy-done.4
  81.2 0.0 copy-done.6
  81.2 0.0 copy-done.8
  81.2 0.0 copy-done.9
  81.2 0.0 copy-done.10
  81.2 4.0 %first.1 = (f32[2,8,64,128]{3,2,1,0:T(8,128)S(1)}, f32[2,8,64,128]{3,2,1,0:T(8,128)S(1)}, f32[256,128]{1,0:T(8,128)S(1)}) custom-call(s32[1]{0:T(128)} %bitcast.dev_ref, f32[2048]{0:T(1024)S(1)} %copy-done.4, f32[8]{0:T(128)S(1)} %copy-done.8, f32[8]{0:T(128)S(1)} %copy-done.9, f32[8]{0:T(128)S(1)} %copy-done.10, f32[3584,128]{1,0:T(8,128)S(1)} %bitcast.7, ...), custom_call_target="tpu_custom_call" | custom-call | tf_op jit(solution)/shard_map/first/pallas_call | solution.py:359
  85.3 0.0 collective-permute-done.k_ref
  85.3 0.0 copy-start.1
  85.3 4.7 %second.1 = f32[2560,128]{1,0:T(8,128)S(1)} custom-call(s32[1]{0:T(128)} %bitcast.dev_ref, f32[2048]{0:T(1024)S(1)} %copy-done.4, f32[8]{0:T(128)S(1)} %copy-done.8, f32[8]{0:T(128)S(1)} %copy-done.9, f32[8]{0:T(128)S(1)} %copy-done.10, f32[3584,128]{1,0:T(8,128)S(1)} %bitcast.8, bf16[256,1024]{1,0:T(8,128)(2,1)S(1)} %copy-done.3, ...), custom_call_target="tpu_custom_call" | custom-call | tf_op jit(solution)/shard_map/second/pallas_call | solution.py:359
  90.0 0.0 copy-start
  90.0 48.1 %all_to_all.19 = f32[512,1,640]{2,1,0:T(1,128)S(1)} all-to-all(f32[512,1,640]{2,1,0:T(1,128)S(1)} %bitcast.10), channel_id=1, replica_groups=mesh['lat_0'=4,'lat_1'=8,'lat_2'=2,'rad_0'=4,'rad_1'=2] {'lat_0','lat_1'..., dimensions={0} | all-to-all | bytes 2621440 | tf_op jit(solution)/shard_map/all_to_all | solution.py:441
  138.1 0.0 copy-done.1
  138.1 0.0 copy-done
  138.1 2.8 %inverse.1 = (f32[16,4,2048]{2,1,0:T(4,128)}, f32[16,4,2048]{2,1,0:T(4,128)}, f32[16,4,2048]{2,1,0:T(4,128)}) custom-call(f32[2560,128]{1,0:T(8,128)S(1)} %bitcast.11, bf16[2,2,512,512]{3,2,1,0:T(8,128)(2,1)S(1)} %copy-done.1, bf16[2,2,512,512]{3,2,1,0:T(8,128)(2,1)S(1)} %copy-done), custom_call_target="tpu_custom_call" | custom-call | tf_op jit(solution)/shard_map/inverse/pallas_call | solution.py:424
  (1 shorter events, 0.0 us)
Async XLA Ops:
  0.6 0.7 copy-start.5
  1.3 0.7 copy-start.7
  78.8 2.4 %copy-start.2 = (bf16[256,1024]{1,0:T(8,128)(2,1)S(1)}, bf16[256,1024]{1,0:T(8,128)(2,1)}, u32[]{:S(2)}) copy-start(bf16[256,1024]{1,0:T(8,128)(2,1)} %constant.43.clone.pl_ref) | copy-start | bytes 1572868
  78.8 2.4 %copy-start.3 = (bf16[256,1024]{1,0:T(8,128)(2,1)S(1)}, bf16[256,1024]{1,0:T(8,128)(2,1)}, u32[]{:S(2)}) copy-start(bf16[256,1024]{1,0:T(8,128)(2,1)} %constant.42.clone.ph_ref) | copy-start | bytes 1572868
  78.8 2.4 %copy-start.4 = (f32[2048]{0:T(1024)S(1)}, f32[2048]{0:T(1024)}, u32[]{:S(2)}) copy-start(f32[2048]{0:T(1024)} %constant.41.clone.gain_ref) | copy-start | bytes 24580
  78.8 2.4 %copy-start.6 = (f32[1,1024]{1,0:T(1,128)S(1)}, f32[1,1024]{1,0:T(1,128)}, u32[]{:S(2)}) copy-start(f32[1,1024]{1,0:T(1,128)} %constant.44.clone.wt_ref) | copy-start | bytes 12292
  78.8 2.4 %copy-start.8 = (f32[8]{0:T(128)S(1)}, f32[8]{0:T(128)}, u32[]{:S(2)}) copy-start(f32[8]{0:T(128)} %mu_ref.3) | copy-start | bytes 100
  78.8 2.4 %copy-start.9 = (f32[8]{0:T(128)S(1)}, f32[8]{0:T(128)}, u32[]{:S(2)}) copy-start(f32[8]{0:T(128)} %dec_ref.3) | copy-start | bytes 100
  78.8 2.4 %copy-start.10 = (f32[8]{0:T(128)S(1)}, f32[8]{0:T(128)}, u32[]{:S(2)}) copy-start(f32[8]{0:T(128)} %con_ref.3) | copy-start | bytes 100
  78.9 6.4 %collective-permute-start = (f32[1024,128]{1,0:T(8,128)S(1)}, f32[1024,128]{1,0:T(8,128)}, u32[]{:S(2)}, u32[]{:S(2)}) collective-permute-start(f32[1024,128]{1,0:T(8,128)S(1)} %half.1), channel_id=1, source_target_pairs={{0,8},{8,0},{1,9},{9,1},{2,10},{10,2},{3,11},{11,3},{4,12},{12,4},... | collective-permute-start | bytes 1572872 | tf_op jit(solution)/shard_map/ppermute | solution.py:458
  85.3 52.8 %copy-start.1 = (bf16[2,2,512,512]{3,2,1,0:T(8,128)(2,1)S(1)}, bf16[2,2,512,512]{3,2,1,0:T(8,128)(2,1)}, u32[]{:S(2)}) copy-start(bf16[2,2,512,512]{3,2,1,0:T(8,128)(2,1)} %constant.39.clone.th_hbm.th_ref) | copy-start | bytes 6291460
  90.0 48.1 %copy-start = (bf16[2,2,512,512]{3,2,1,0:T(8,128)(2,1)S(1)}, bf16[2,2,512,512]{3,2,1,0:T(8,128)(2,1)}, u32[]{:S(2)}) copy-start(bf16[2,2,512,512]{3,2,1,0:T(8,128)(2,1)} %constant.40.clone.tl_hbm.tl_ref) | copy-start | bytes 6291460

commit v4 on v3

--- a/solution.py
+++ b/solution.py
@@ -89,16 +89,19 @@
 
 
 def forward_kernel(
-    u_hbm, q_hbm, ice_hbm, th_hbm, tl_hbm, mat_ref, ker_ref, a_ref, x_ref, w_ref, f_ref, ice_ref, th_ref, tl_ref, sem
+    u_hbm, q_hbm, ice_hbm, mat_hbm, ker_hbm, th_hbm, tl_hbm, a_ref,
+    x_ref, w_ref, f_ref, ice_ref, mat_ref, ker_ref, th_ref, tl_ref, sem,
 ):
     copies = [
         pltpu.make_async_copy(u_hbm, f_ref.at[0], sem.at[0]),
         pltpu.make_async_copy(q_hbm, f_ref.at[1], sem.at[1]),
         pltpu.make_async_copy(ice_hbm, ice_ref, sem.at[2]),
+        pltpu.make_async_copy(mat_hbm, mat_ref, sem.at[3]),
+        pltpu.make_async_copy(ker_hbm, ker_ref, sem.at[4]),
     ]
     for k2 in range(2):
         for e in range(2):
-            n = 3 + 4 * k2 + 2 * e
+            n = 5 + 4 * k2 + 2 * e
             copies.append(pltpu.make_async_copy(th_hbm.at[k2, e], th_ref.at[k2, e], sem.at[n]))
             copies.append(pltpu.make_async_copy(tl_hbm.at[k2, e], tl_ref.at[k2, e], sem.at[n + 1]))
     for copy in copies:
@@ -106,6 +109,9 @@
     peer = lax.broadcasted_iota(jnp.int32, (DEV, 128), 0)
     lane = lax.broadcasted_iota(jnp.int32, (DEV, 128), 1)
     core = (peer >> 3) & 1
+    x_ref[:, :, 256:, :] = jnp.zeros((2, 2, 128, QUART), BF16)
+    copies[3].wait()
+    copies[4].wait()
     ker = jnp.concatenate([ker_ref[:, rr, :] for rr in range(NK)], axis=1)
     for t in range(2):
         a_ref[pl.ds(5 + t, DEV, stride=RIN), :] = jnp.where(core == 0, ker[t : t + 1], ker[2 + t : 3 + t])
@@ -115,7 +121,6 @@
     mat = dot_nn(mat_ref[...].astype(F32).astype(BF16), spread)
     mat = jnp.where((lane[:NK] & 3) == peer[:NK], mat, 0.0)
     extra = jnp.broadcast_to(jnp.sum(mat, axis=0, keepdims=True), (DEV, 128))
-    x_ref[:, :, 256:, :] = jnp.zeros((2, 2, 128, QUART), BF16)
     for f in range(2):
         copies[f].wait()
         for j in range(NJ):
@@ -147,7 +152,7 @@
     for k2 in range(2):
         product = []
         for e in range(2):
-            n = 3 + 4 * k2 + 2 * e
+            n = 5 + 4 * k2 + 2 * e
             copies[n].wait()
             copies[n + 1].wait()
             x = x_ref[k2, e]
@@ -167,10 +172,10 @@
 def forward(u, q, ice, mat, ker, th, tl):
     hbm = pl.BlockSpec(memory_space=pltpu.MemorySpace.HBM)
     vmem = pl.BlockSpec(memory_space=pltpu.VMEM)
-    far = [pltpu.with_memory_space_constraint(x, pltpu.MemorySpace.HBM) for x in (u, q, ice, th, tl)]
+    far = [pltpu.with_memory_space_constraint(x, pltpu.MemorySpace.HBM) for x in (u, q, ice, mat, ker, th, tl)]
     return pl.pallas_call(
         forward_kernel,
-        in_specs=[hbm] * 5 + [vmem] * 2,
+        in_specs=[hbm] * 7,
         out_specs=vmem,
         out_shape=jax.ShapeDtypeStruct((DEV * RIN, 128), F32),
         scratch_shapes=[
@@ -178,13 +183,15 @@
             pltpu.VMEM((128 + NJ, NLON), F32),
             pltpu.VMEM((2, NJ, NK, NLON), F32),
             pltpu.VMEM((NJ, NLON), jnp.int32),
+            pltpu.VMEM((NK, NJ), jnp.int32),
+            pltpu.VMEM((4, NK, NR), F32),
             pltpu.VMEM((2, 2, DEV, QUART), BF16),
             pltpu.VMEM((2, 2, DEV, QUART), BF16),
-            pltpu.SemaphoreType.DMA((11,)),
+            pltpu.SemaphoreType.DMA((13,)),
         ],
-        compiler_params=pltpu.CompilerParams(vmem_limit_bytes=48 << 20),
+        compiler_params=pltpu.CompilerParams(vmem_limit_bytes=24 << 20),
         name="forward",
-    )(*far, mat, ker)
+    )(*far)
 
 
 def lane_tables():
@@ -214,15 +221,14 @@
         stiff = look(mu_ref)
         st_ref[b] = stiff
         dc_ref[b] = look(dec_ref)
-        if r_ref is not None:
-            r_ref[b] = look(con_ref)
+        r_ref[b] = look(con_ref)
         g_ref[b] = (RELAX / DIAG) / stiff
         layer = (r + (4 * b + 1)).astype(F32) * (LOAD / NR)
         for kk in range(2):
             s_ref[kk, b] = take(extra, kk * 32 + (lane >> 2)) * layer
 
 
-def three_sweeps(p, gain_ref, u_ref, q_ref, s_ref, st_ref, dc_ref, g_ref):
+def three_sweeps(p, gain_ref, bufs, q_ref, q_out, s_ref, st_ref, dc_ref, g_ref):
     shape, lane, row = lane_tables()
     r = lane & 3
     j = (lane >> 2) & 15
@@ -232,26 +238,26 @@
     jm = (lane & 64) | ((lane + 60) & 63)
     gains = [jnp.where(lane < 64, gain_ref[4 * p + 2 * kk], gain_ref[4 * p + 2 * kk + 1]) for kk in range(2)]
     zero = jnp.zeros(shape, F32)
-    for buf in range(2):
+    for buf in bufs[1:]:
         for kk in range(2):
-            u_ref[buf, kk, 0] = zero
-            u_ref[buf, kk, NB + 1] = zero
-
+            buf[kk, 0] = zero
+            buf[kk, NB + 1] = zero
     for step in range(3):
-        src, dst = step % 2, 1 - step % 2
+        src, dst = bufs[step], bufs[step + 1]
+        q_src = q_ref if step == 0 else q_out
         for kk in range(2):
             for b in range(NB):
-                uc = u_ref[src, kk, b + 1]
-                up = u_ref[src, kk, b + 2]
-                dn = u_ref[src, kk, b]
+                uc = src[kk, b + 1]
+                up = src[kk, b + 2]
+                dn = src[kk, b]
                 ip = jnp.where(row == NI - 1, 0.0, pltpu.roll(uc, NI - 1, 0))
                 im = jnp.where(row == 0, 0.0, pltpu.roll(uc, 1, 0))
                 beside = take(jnp.where(r == 0, up, uc), rp) + take(jnp.where(r == 3, dn, uc), rm)
                 beside = beside + take(jnp.where(j == 0, ip, uc), jp) + take(jnp.where(j == 15, im, uc), jm)
-                q = q_ref[kk, b]
+                q = q_src[kk, b]
                 un = gains[kk] * uc + g_ref[b] * (s_ref[kk, b] - q) + (RELAX / DIAG) * beside
-                u_ref[dst, kk, b + 1] = un
-                q_ref[kk, b] = dc_ref[b] * q + st_ref[b] * (un - uc)
+                dst[kk, b + 1] = un
+                q_out[kk, b] = dc_ref[b] * q + st_ref[b] * (un - uc)
 
 
 def half_kernel(b_ref, o_ref):
@@ -260,22 +266,23 @@
 
 
 def first_kernel(
-    dev_ref, gain_ref, mu_ref, dec_ref, con_ref, b_ref, ph_ref, pl_ref, wt_ref, u3_ref, q_ref, c_ref,
-    u_ref, s_ref, st_ref, dc_ref, g_ref, r_ref, z_ref, rt_ref,
+    dev_ref, gain_ref, mu_ref, dec_ref, con_ref, b_ref, ph_ref, pl_ref, wt_ref,
+    u3_ref, q_ref, s_ref, st_ref, dc_ref, g_ref, c_ref,
+    ua_ref, ub_ref, r_ref, z_ref, rt_ref,
 ):
     p = dev_ref[0]
     par = p % 2
     load_materials(b_ref, mu_ref, dec_ref, con_ref, s_ref, st_ref, dc_ref, g_ref, r_ref)
-    for b in range(NB):
-        for kk in range(2):
-            u_ref[0, kk, b + 1] = b_ref[pl.ds(b * RIN + kk, NI, stride=NB * RIN), :]
+    for kk in range(2):
+        ua_ref[kk, 0] = jnp.zeros((NI, 128), F32)
+        ua_ref[kk, NB + 1] = jnp.zeros((NI, 128), F32)
+        for b in range(NB):
+            ua_ref[kk, b + 1] = b_ref[pl.ds(b * RIN + kk, NI, stride=NB * RIN), :]
             q_ref[kk, b] = b_ref[pl.ds(b * RIN + 2 + kk, NI, stride=NB * RIN), :]
-    three_sweeps(p, gain_ref, u_ref, q_ref, s_ref, st_ref, dc_ref, g_ref)
-    for b in range(NB):
-        for kk in range(2):
-            u3_ref[kk, b] = u_ref[1, kk, b + 1]
+    bufs = (ua_ref, ub_ref, ua_ref, u3_ref)
+    three_sweeps(p, gain_ref, bufs, q_ref, q_ref, s_ref, st_ref, dc_ref, g_ref)
     for h in range(NB // 2):
-        pair = [r_ref[2 * h + t] * u_ref[1, 0, 2 * h + t + 1] for t in range(2)]
+        pair = [r_ref[2 * h + t] * u3_ref[0, 2 * h + t + 1] for t in range(2)]
         rt_ref[:, 128 * h : 128 * h + 128] = jnp.concatenate(pair, axis=0).T
     kept = rt_ref[pl.ds(pl.multiple_of(64 * par, 64), 64), :]
     for jj in range(NJ):
@@ -292,19 +299,14 @@
 
 
 def second_kernel(
-    dev_ref, gain_ref, mu_ref, dec_ref, con_ref, b_ref, ph_ref, pl_ref, u3_ref, q3_ref, c_ref, k_ref, o_ref,
-    u_ref, q_ref, s_ref, st_ref, dc_ref, g_ref, rt_ref, phi_ref,
+    dev_ref, gain_ref, b_ref, ph_ref, pl_ref, u3_ref, q3_ref, s3_ref, st_ref, dc_ref, g_ref, c_ref, k_ref, o_ref,
+    ua_ref, ub_ref, q_ref, s_ref, rt_ref, phi_ref,
 ):
     p = dev_ref[0]
     par = p % 2
     core = (p // NB) % 2
     mine = pl.multiple_of(128 * core, 128)
     other = pl.multiple_of(128 - 128 * core, 128)
-    load_materials(b_ref, mu_ref, dec_ref, con_ref, s_ref, st_ref, dc_ref, g_ref, None)
-    for b in range(NB):
-        for kk in range(2):
-            u_ref[0, kk, b + 1] = u3_ref[kk, b]
-            q_ref[kk, b] = q3_ref[kk, b]
     lane1 = lax.broadcasted_iota(jnp.int32, (128, 128), 1)
     sub1 = lax.broadcasted_iota(jnp.int32, (128, 128), 0)
     phi = jnp.zeros((NDEG, 128), F32)
@@ -342,11 +344,13 @@
             b = 2 * h + t
             piece = back[64 * t : 64 * t + 64]
             o_ref[pl.ds(b * ROUT + 4, NI, stride=NB * ROUT), :] = piece
-            s_ref[0, b] = s_ref[0, b] + COUPLE * piece
-    three_sweeps(p, gain_ref, u_ref, q_ref, s_ref, st_ref, dc_ref, g_ref)
+            s_ref[0, b] = s3_ref[0, b] + COUPLE * piece
+            s_ref[1, b] = s3_ref[1, b]
+    bufs = (u3_ref, ua_ref, ub_ref, ua_ref)
+    three_sweeps(p, gain_ref, bufs, q3_ref, q_ref, s_ref, st_ref, dc_ref, g_ref)
     for b in range(NB):
         for kk in range(2):
-            o_ref[pl.ds(b * ROUT + kk, NI, stride=NB * ROUT), :] = u_ref[1, kk, b + 1]
+            o_ref[pl.ds(b * ROUT + kk, NI, stride=NB * ROUT), :] = ua_ref[kk, b + 1]
             o_ref[pl.ds(b * ROUT + 2 + kk, NI, stride=NB * ROUT), :] = q_ref[kk, b]
 
 
@@ -362,7 +366,7 @@
         out_specs=jax.tree.map(lambda _: vmem, out_shape),
         out_shape=out_shape,
         scratch_shapes=[pltpu.VMEM(shape, F32) for shape in scratch],
-        compiler_params=pltpu.CompilerParams(vmem_limit_bytes=48 << 20),
+        compiler_params=pltpu.CompilerParams(vmem_limit_bytes=16 << 20),
         name=name,
     )(*scalars, *arrays)
 
@@ -431,7 +435,7 @@
             pltpu.VMEM((3, *shape), F32),
             pltpu.SemaphoreType.DMA((2, 3, 2)),
         ],
-        compiler_params=pltpu.CompilerParams(vmem_limit_bytes=48 << 20),
+        compiler_params=pltpu.CompilerParams(vmem_limit_bytes=16 << 20),
         name="inverse",
     )(b, th, tl)
 
@@ -458,19 +462,17 @@
         swapped = lax.ppermute(half, "lat_2", [(0, 1), (1, 0)])
         scalars = (dev, jnp.asarray(gain_np), mu_table, decay_table, contrast_table)
         ph, plo = jnp.asarray(ph_np), jnp.asarray(pl_np)
-        u3, q3, coef = local_call(
+        padded, field = (2, NB + 2, NI, 128), (2, *FIELD)
+        shapes = (padded, field, field, FIELD, FIELD, FIELD, (NDEG, 128))
+        state = local_call(
             first_kernel, "first", scalars, (arrived, ph, plo, jnp.asarray(wt_np)),
-            [
-                jax.ShapeDtypeStruct((2, *FIELD), F32),
-                jax.ShapeDtypeStruct((2, *FIELD), F32),
-                jax.ShapeDtypeStruct((NDEG, 128), F32),
-            ],
-            [(2, 2, NB + 2, NI, 128), (2, *FIELD), FIELD, FIELD, FIELD, FIELD, (NR, NLAT), (128, DEV)],
+            [jax.ShapeDtypeStruct(shape, F32) for shape in shapes],
+            [padded, padded, FIELD, (NR, NLAT), (128, DEV)],
         )
         moved = local_call(
-            second_kernel, "second", scalars, (arrived, ph, plo, u3, q3, coef, swapped),
+            second_kernel, "second", scalars[:2], (arrived, ph, plo, *state, swapped),
             jax.ShapeDtypeStruct((DEV * ROUT, 128), F32),
-            [(2, 2, NB + 2, NI, 128), (2, *FIELD), (2, *FIELD), FIELD, FIELD, FIELD, (128, DEV), (NDEG, 128)],
+            [padded, padded, field, field, (128, DEV), (NDEG, 128)],
         )
         returned = exchange(moved, ROUT)
         return tuple(inverse(returned, th, tl))

time: 141 us -> 140 us (level)
  no operation moved by 1% of the time
where the time goes in v4:
time: 140 us
  blocking collectives  120 us (86%)
  Pallas kernels  16.6 us (12%)
  starting transfers between devices  1.95 us (1%)
    all_to_all x2, blocking collectives, exchange(): x = lax.all_to_all(x, ALL, split_axis=0, concat_axis=0, tiled=True)  120 us
    pallas_call x3, Pallas kernels, local_call(): pl.pallas_call(kernel, in_specs=[smem] * len(scalars) + [vmem] * len(arra...  8.97 us
    pallas_call x1, Pallas kernels, forward(): pl.pallas_call(forward_kernel, in_specs=[hbm] * 7, out_specs=vmem, out_sh...  4.88 us
  transfers between devices with their start and end apart: 1, of which 0 were waited for; matrix products, arithmetic and copies ran while one was open for 0% of the time, Pallas kernels for 3%

profile of v4, /device:TPU:1, one launch (start us, length us, event | category | flops | bytes accessed | tf_op | source)
XLA Modules:
  0.0 139.8 jit_solution(4587490224900555260)
XLA Ops:
  0.6 4.9 %forward.1 = f32[3584,128]{1,0:T(8,128)S(1)} custom-call(f32[16,4,2048]{2,1,0:T(4,128)} %u_hbm.1, f32[16,4,2048]{2,1,0:T(4,128)} %q_hbm.1, s32[16,2048]{1,0:T(8,128)} %ice_hbm.1, s32[4,16]{1,0:T(4,128)} %bitcast.12, f32[4,4,32]{2,1,0:T(4,128)} %ker_hbm.1, bf16[2,2,512,512]{3,2,1,0:T(8,128)(2,1)} %constant.39.clone.th_hbm.th_ref, ...), custom_call_target="tpu_custom_call" | custom-call | tf_op jit(solution)/shard_map/forward/pallas_call | solution.py:176
  5.5 72.0 %all_to_all.18 = f32[512,1,896]{2,1,0:T(1,128)S(1)} all-to-all(f32[512,1,896]{2,1,0:T(1,128)S(1)} %bitcast.9), channel_id=1, replica_groups=mesh['lat_0'=4,'lat_1'=8,'lat_2'=2,'rad_0'=4,'rad_1'=2] {'lat_0','lat_1'..., dimensions={0} | all-to-all | bytes 3670016 | tf_op jit(solution)/shard_map/all_to_all | solution.py:445
  77.5 0.0 copy-start.2
  77.5 0.0 copy-start.3
  77.5 0.0 copy-start.4
  77.5 0.0 copy-start.5
  77.5 0.0 copy-start.6
  77.5 0.0 copy-start.7
  77.5 0.0 copy-start.8
  77.5 0.8 half.1
  78.4 1.9 %collective-permute-start = (f32[1024,128]{1,0:T(8,128)}, f32[1024,128]{1,0:T(8,128)S(1)}, u32[]{:S(2)}, u32[]{:S(2)}) collective-permute-start(f32[1024,128]{1,0:T(8,128)} %half.1), channel_id=1, source_target_pairs={{0,8},{8,0},{1,9},{9,1},{2,10},{10,2},{3,11},{11,3},{4,12},{12,4},... | collective-permute-start | bytes 1572872 | tf_op jit(solution)/shard_map/ppermute | solution.py:462
  80.3 0.0 copy-done.2
  80.3 0.0 copy-done.3
  80.3 0.0 copy-done.4
  80.4 0.0 copy-done.5
  80.4 0.0 copy-done.6
  80.4 0.0 copy-done.7
  80.4 0.0 copy-done.8
  80.4 4.2 %first.1 = (f32[2,10,64,128]{3,2,1,0:T(8,128)S(1)}, f32[2,8,64,128]{3,2,1,0:T(8,128)S(1)}, f32[2,8,64,128]{3,2,1,0:T(8,128)S(1)}, f32[8,64,128]{2,1,0:T(8,128)S(...) custom-call(s32[1]{0:T(128)} %bitcast.dev_ref, f32[2048]{0:T(1024)S(1)} %copy-done.4, ...), custom_call_target="tpu_custom_call" | custom-call | tf_op jit(solution)/shard_map/first/pallas_call | solution.py:363
  84.6 0.0 collective-permute-done.k_ref
  84.6 0.0 copy-start.1
  84.6 4.0 %second.1 = f32[2560,128]{1,0:T(8,128)S(1)} custom-call(s32[1]{0:T(128)} %bitcast.dev_ref, f32[2048]{0:T(1024)S(1)} %copy-done.4, f32[3584,128]{1,0:T(8,128)S(1)} %bitcast.8, bf16[256,1024]{1,0:T(8,128)(2,1)S(1)} %copy-done.3, bf16[256,1024]{1,0:T(8,128)(2,1)S(1)} %copy-done.2, f32[2,10,64,128]{3,2,1,0:T(8,128)S(1)} %get-tuple-element.10.u3_ref, ...), custom_call_target="tpu_custom_call" | custom-call | tf_op jit(solution)/shard_map/second/pallas_call | solution.py:363
  88.6 0.0 copy-start
  88.6 48.2 %all_to_all.19 = f32[512,1,640]{2,1,0:T(1,128)S(1)} all-to-all(f32[512,1,640]{2,1,0:T(1,128)S(1)} %bitcast.10), channel_id=1, replica_groups=mesh['lat_0'=4,'lat_1'=8,'lat_2'=2,'rad_0'=4,'rad_1'=2] {'lat_0','lat_1'..., dimensions={0} | all-to-all | bytes 2621440 | tf_op jit(solution)/shard_map/all_to_all | solution.py:445
  136.8 0.0 copy-done.1
  136.8 0.0 copy-done
  136.8 2.8 %inverse.1 = (f32[16,4,2048]{2,1,0:T(4,128)}, f32[16,4,2048]{2,1,0:T(4,128)}, f32[16,4,2048]{2,1,0:T(4,128)}) custom-call(f32[2560,128]{1,0:T(8,128)S(1)} %bitcast.11, bf16[2,2,512,512]{3,2,1,0:T(8,128)(2,1)S(1)} %copy-done.1, bf16[2,2,512,512]{3,2,1,0:T(8,128)(2,1)S(1)} %copy-done), custom_call_target="tpu_custom_call" | custom-call | tf_op jit(solution)/shard_map/inverse/pallas_call | solution.py:428
Async XLA Ops:
  77.5 2.8 %copy-start.2 = (bf16[256,1024]{1,0:T(8,128)(2,1)S(1)}, bf16[256,1024]{1,0:T(8,128)(2,1)}, u32[]{:S(2)}) copy-start(bf16[256,1024]{1,0:T(8,128)(2,1)} %constant.43.clone.pl_ref) | copy-start | bytes 1572868
  77.5 2.9 %copy-start.3 = (bf16[256,1024]{1,0:T(8,128)(2,1)S(1)}, bf16[256,1024]{1,0:T(8,128)(2,1)}, u32[]{:S(2)}) copy-start(bf16[256,1024]{1,0:T(8,128)(2,1)} %constant.42.clone.ph_ref) | copy-start | bytes 1572868
  77.5 2.9 %copy-start.4 = (f32[2048]{0:T(1024)S(1)}, f32[2048]{0:T(1024)}, u32[]{:S(2)}) copy-start(f32[2048]{0:T(1024)} %constant.41.clone.gain_ref) | copy-start | bytes 24580
  77.5 2.9 %copy-start.5 = (f32[1,1024]{1,0:T(1,128)S(1)}, f32[1,1024]{1,0:T(1,128)}, u32[]{:S(2)}) copy-start(f32[1,1024]{1,0:T(1,128)} %constant.44.clone.wt_ref) | copy-start | bytes 12292
  77.5 2.9 %copy-start.6 = (f32[8]{0:T(128)S(1)}, f32[8]{0:T(128)}, u32[]{:S(2)}) copy-start(f32[8]{0:T(128)} %mu_ref.1) | copy-start | bytes 100
  77.5 2.9 %copy-start.7 = (f32[8]{0:T(128)S(1)}, f32[8]{0:T(128)}, u32[]{:S(2)}) copy-start(f32[8]{0:T(128)} %dec_ref.1) | copy-start | bytes 100
  77.5 2.9 %copy-start.8 = (f32[8]{0:T(128)S(1)}, f32[8]{0:T(128)}, u32[]{:S(2)}) copy-start(f32[8]{0:T(128)} %con_ref.1) | copy-start | bytes 100
  78.4 6.2 %collective-permute-start = (f32[1024,128]{1,0:T(8,128)}, f32[1024,128]{1,0:T(8,128)S(1)}, u32[]{:S(2)}, u32[]{:S(2)}) collective-permute-start(f32[1024,128]{1,0:T(8,128)} %half.1), channel_id=1, source_target_pairs={{0,8},{8,0},{1,9},{9,1},{2,10},{10,2},{3,11},{11,3},{4,12},{12,4},... | collective-permute-start | bytes 1572872 | tf_op jit(solution)/shard_map/ppermute | solution.py:462
  84.6 52.3 %copy-start.1 = (bf16[2,2,512,512]{3,2,1,0:T(8,128)(2,1)S(1)}, bf16[2,2,512,512]{3,2,1,0:T(8,128)(2,1)}, u32[]{:S(2)}) copy-start(bf16[2,2,512,512]{3,2,1,0:T(8,128)(2,1)} %constant.39.clone.th_hbm.th_ref) | copy-start | bytes 6291460
  88.6 48.3 %copy-start = (bf16[2,2,512,512]{3,2,1,0:T(8,128)(2,1)S(1)}, bf16[2,2,512,512]{3,2,1,0:T(8,128)(2,1)}, u32[]{:S(2)}) copy-start(bf16[2,2,512,512]{3,2,1,0:T(8,128)(2,1)} %constant.40.clone.tl_hbm.tl_ref) | copy-start | bytes 6291460

commit v5 on v4

--- a/solution.py
+++ b/solution.py
@@ -129,37 +129,39 @@
     w_ref[pl.ds(128, NJ), :] = ice_ref[...].astype(F32)
     rows = 128 + NJ
     parity = lax.broadcasted_iota(jnp.int32, (rows, 128), 1) & 1
-    for m in range(HALF // 256):
-        parts = []
-        for t in range(2):
-            start = 256 * m + 128 * t
-            low, high = w_ref[:, start : start + 128], w_ref[:, HALF + start : HALF + start + 128]
-            parts.append((low + high, low - high))
-        for k2 in range(2):
-            v0, v1 = parts[0][k2], parts[1][k2]
+    def build(k2):
+        for m in range(HALF // 256):
+            v = []
+            for t in range(2):
+                start = 256 * m + 128 * t
+                low, high = w_ref[:, start : start + 128], w_ref[:, HALF + start : HALF + start + 128]
+                v.append(low + high if k2 == 0 else low - high)
             for e, value in (
-                (0, jnp.where(parity == 0, v0, pltpu.roll(v1, 1, 1))),
-                (1, jnp.where(parity == 0, pltpu.roll(v0, 127, 1), v1)),
+                (0, jnp.where(parity == 0, v[0], pltpu.roll(v[1], 1, 1))),
+                (1, jnp.where(parity == 0, pltpu.roll(v[0], 127, 1), v[1])),
             ):
                 hi, lo = split(value[:128])
                 cols = slice(128 * m, 128 * m + 128)
                 x_ref[k2, e, 0:128, cols] = lo
                 x_ref[k2, e, 128:256, cols] = hi
                 x_ref[k2, e, 256 + NJ * k2 : 256 + NJ * k2 + NJ, cols] = value[128:].astype(BF16)
+
     first = lane < 64
     slots = []
     ice_sum = [0.0, 0.0]
+    build(0)
     for k2 in range(2):
+        for copy in copies[5 + 4 * k2 : 9 + 4 * k2]:
+            copy.wait()
         product = []
         for e in range(2):
-            n = 5 + 4 * k2 + 2 * e
-            copies[n].wait()
-            copies[n + 1].wait()
             x = x_ref[k2, e]
             r1 = dot_nt(th_ref[k2, e], x)
             r2 = dot_nt(tl_ref[k2, e], x[128:])
             product.append(r1[:, 128:256] + (r1[:, :128] + r2[:, :128]))
             ice_sum[e] = ice_sum[e] + (r1[:, 256:] + r2[:, 128:])
+        if k2 == 0:
+            build(1)
         slots.append((product[0] + product[1], product[0] - product[1]))
     for kk in range(2):
         even, odd = slots[0][kk], slots[1][kk]
@@ -307,26 +309,28 @@
     core = (p // NB) % 2
     mine = pl.multiple_of(128 * core, 128)
     other = pl.multiple_of(128 - 128 * core, 128)
-    lane1 = lax.broadcasted_iota(jnp.int32, (128, 128), 1)
-    sub1 = lax.broadcasted_iota(jnp.int32, (128, 128), 0)
-    phi = jnp.zeros((NDEG, 128), F32)
     coef_mine = c_ref[pl.ds(mine, 128), :]
     coef_other = c_ref[pl.ds(other, 128), :]
+    products = []
     for b in range(NB):
-        prod = jnp.concatenate(
-            [
-                b_ref[pl.ds(b * RIN + 5 + t, NI, stride=NB * RIN), :] * coef_mine[64 * t : 64 * t + 64]
-                for t in range(2)
-            ]
-            + [
-                k_ref[pl.ds(t * DEV + b, NI, stride=NB), :] * coef_other[64 * t : 64 * t + 64]
-                for t in range(2)
-            ],
-            axis=0,
+        products.append(
+            jnp.concatenate(
+                [
+                    b_ref[pl.ds(b * RIN + 5 + t, NI, stride=NB * RIN), :] * coef_mine[64 * t : 64 * t + 64]
+                    for t in range(2)
+                ]
+                + [
+                    k_ref[pl.ds(t * DEV + b, NI, stride=NB), :] * coef_other[64 * t : 64 * t + 64]
+                    for t in range(2)
+                ],
+                axis=0,
+            )
         )
-        pick = (lane1 == (sub1 >> 5) + 4 * b).astype(BF16)
-        hi, lo = split(prod)
-        phi = phi + (dot_nn(hi, pick) + dot_nn(lo, pick))
+    lane1 = lax.broadcasted_iota(jnp.int32, (128 * NB, 128), 1)
+    sub1 = lax.broadcasted_iota(jnp.int32, (128 * NB, 128), 0)
+    pick = (lane1 == (sub1 >> 5)).astype(BF16)
+    hi, lo = split(jnp.concatenate(products, axis=1))
+    phi = dot_nn(hi, pick) + dot_nn(lo, pick)
     factor = jnp.where(p == 0, 2.0, jnp.where(p == MODES, 0.0, 1.0))
     phi_ref[pl.ds(mine, 128), :] = phi[:128] * factor
     phi_ref[pl.ds(other, 128), :] = phi[128:] * factor
@@ -380,7 +384,7 @@
             for k2 in range(2):
                 y_ref[k2, e, 64 * f : 64 * f + 64, :] = hi[64 * k2 : 64 * k2 + 64]
                 y_ref[k2, e, 192 + 64 * f : 256 + 64 * f, :] = lo[64 * k2 : 64 * k2 + 64]
-    parity = lax.broadcasted_iota(jnp.int32, (192, 128), 1) & 1
+    parity = lax.broadcasted_iota(jnp.int32, (64, 128), 1) & 1
     copies = []
     for n in range(2):
         cols = slice(256 * n, 256 * n + 256)
@@ -393,25 +397,23 @@
                 r1 = dot_nn(y, th)
                 made.append(r1[:192] + (r1[192:] + dot_nn(y[:192], tl)))
             halves.append(made)
-        for t in range(2):
-            m = 2 * n + t
-            both = []
-            for k2 in range(2):
-                even, odd = (x[:, 128 * t : 128 * t + 128] for x in halves[k2])
-                both.append(
-                    (
-                        jnp.where(parity == 0, even, pltpu.roll(odd, 1, 1)),
-                        jnp.where(parity == 0, pltpu.roll(even, 127, 1), odd),
+        for f, ref in enumerate((u_hbm, q_hbm, p_hbm)):
+            rows = slice(64 * f, 64 * f + 64)
+            for t in range(2):
+                both = []
+                for k2 in range(2):
+                    even, odd = (x[rows, 128 * t : 128 * t + 128] for x in halves[k2])
+                    both.append(
+                        (
+                            jnp.where(parity == 0, even, pltpu.roll(odd, 1, 1)),
+                            jnp.where(parity == 0, pltpu.roll(even, 127, 1), odd),
+                        )
                     )
-                )
-            for v in range(2):
-                for base, value in ((0, both[0][v] + both[1][v]), (HALF, both[0][v] - both[1][v])):
-                    start = base + 256 * m + 128 * v
-                    for f in range(3):
+                for v in range(2):
+                    start = 512 * n + 256 * t + 128 * v
+                    for base, value in ((0, both[0][v] + both[1][v]), (HALF, both[0][v] - both[1][v])):
                         for j in range(NJ):
-                            row = 64 * f + 4 * j
-                            out_ref[f, j, :, start : start + 128] = value[row : row + 4]
-        for f, ref in enumerate((u_hbm, q_hbm, p_hbm)):
+                            out_ref[f, j, :, base + start : base + start + 128] = value[4 * j : 4 * j + 4]
             for h in range(2):
                 span = pl.ds(HALF * h + 512 * n, 512)
                 copy = pltpu.make_async_copy(out_ref.at[f, :, :, span], ref.at[:, :, span], sem.at[n, f, h])

time: 140 us -> 139 us (level)
  no operation moved by 1% of the time
where the time goes in v5:
time: 139 us
  blocking collectives  120 us (86%)
  Pallas kernels  15.8 us (11%)
  starting transfers between devices  1.95 us (1%)
    all_to_all x2, blocking collectives, exchange(): x = lax.all_to_all(x, ALL, split_axis=0, concat_axis=0, tiled=True)  120 us
    pallas_call x3, Pallas kernels, local_call(): pl.pallas_call(kernel, in_specs=[smem] * len(scalars) + [vmem] * len(arra...  8.86 us
    pallas_call x1, Pallas kernels, forward(): pl.pallas_call(forward_kernel, in_specs=[hbm] * 7, out_specs=vmem, out_sh...  4.17 us
  transfers between devices with their start and end apart: 1, of which 0 were waited for; matrix products, arithmetic and copies ran while one was open for 0% of the time, Pallas kernels for 3%

profile of v5, /device:TPU:1, one launch (start us, length us, event | category | flops | bytes accessed | tf_op | source)
XLA Modules:
  0.0 138.9 jit_solution(14149386771400427223)
XLA Ops:
  0.6 4.2 %forward.1 = f32[3584,128]{1,0:T(8,128)S(1)} custom-call(f32[16,4,2048]{2,1,0:T(4,128)} %u_hbm.1, f32[16,4,2048]{2,1,0:T(4,128)} %q_hbm.1, s32[16,2048]{1,0:T(8,128)} %ice_hbm.1, s32[4,16]{1,0:T(4,128)} %bitcast.12, f32[4,4,32]{2,1,0:T(4,128)} %ker_hbm.1, bf16[2,2,512,512]{3,2,1,0:T(8,128)(2,1)} %constant.39.clone.th_hbm.th_ref, ...), custom_call_target="tpu_custom_call" | custom-call | tf_op jit(solution)/shard_map/forward/pallas_call | solution.py:178
  4.8 72.0 %all_to_all.18 = f32[512,1,896]{2,1,0:T(1,128)S(1)} all-to-all(f32[512,1,896]{2,1,0:T(1,128)S(1)} %bitcast.9), channel_id=1, replica_groups=mesh['lat_0'=4,'lat_1'=8,'lat_2'=2,'rad_0'=4,'rad_1'=2] {'lat_0','lat_1'..., dimensions={0} | all-to-all | bytes 3670016 | tf_op jit(solution)/shard_map/all_to_all | solution.py:447
  76.8 0.0 copy-start.2
  76.8 0.0 copy-start.3
  76.8 0.0 copy-start.4
  76.8 0.0 copy-start.5
  76.8 0.0 copy-start.6
  76.8 0.0 copy-start.7
  76.8 0.0 copy-start.8
  76.8 0.8 half.1
  77.7 1.9 %collective-permute-start = (f32[1024,128]{1,0:T(8,128)}, f32[1024,128]{1,0:T(8,128)S(1)}, u32[]{:S(2)}, u32[]{:S(2)}) collective-permute-start(f32[1024,128]{1,0:T(8,128)} %half.1), channel_id=1, source_target_pairs={{0,8},{8,0},{1,9},{9,1},{2,10},{10,2},{3,11},{11,3},{4,12},{12,4},... | collective-permute-start | bytes 1572872 | tf_op jit(solution)/shard_map/ppermute | solution.py:464
  79.6 0.0 copy-done.2
  79.6 0.0 copy-done.3
  79.6 0.0 copy-done.4
  79.7 0.0 copy-done.5
  79.7 0.0 copy-done.6
  79.7 0.0 copy-done.7
  79.7 0.0 copy-done.8
  79.7 4.2 %first.1 = (f32[2,10,64,128]{3,2,1,0:T(8,128)S(1)}, f32[2,8,64,128]{3,2,1,0:T(8,128)S(1)}, f32[2,8,64,128]{3,2,1,0:T(8,128)S(1)}, f32[8,64,128]{2,1,0:T(8,128)S(...) custom-call(s32[1]{0:T(128)} %bitcast.dev_ref, f32[2048]{0:T(1024)S(1)} %copy-done.4, ...), custom_call_target="tpu_custom_call" | custom-call | tf_op jit(solution)/shard_map/first/pallas_call | solution.py:367
  83.8 0.0 collective-permute-done.k_ref
  83.9 0.0 copy-start.1
  83.9 3.9 %second.1 = f32[2560,128]{1,0:T(8,128)S(1)} custom-call(s32[1]{0:T(128)} %bitcast.dev_ref, f32[2048]{0:T(1024)S(1)} %copy-done.4, f32[3584,128]{1,0:T(8,128)S(1)} %bitcast.8, bf16[256,1024]{1,0:T(8,128)(2,1)S(1)} %copy-done.3, bf16[256,1024]{1,0:T(8,128)(2,1)S(1)} %copy-done.2, f32[2,10,64,128]{3,2,1,0:T(8,128)S(1)} %get-tuple-element.10.u3_ref, ...), custom_call_target="tpu_custom_call" | custom-call | tf_op jit(solution)/shard_map/second/pallas_call | solution.py:367
  87.8 0.0 copy-start
  87.8 48.2 %all_to_all.19 = f32[512,1,640]{2,1,0:T(1,128)S(1)} all-to-all(f32[512,1,640]{2,1,0:T(1,128)S(1)} %bitcast.10), channel_id=1, replica_groups=mesh['lat_0'=4,'lat_1'=8,'lat_2'=2,'rad_0'=4,'rad_1'=2] {'lat_0','lat_1'..., dimensions={0} | all-to-all | bytes 2621440 | tf_op jit(solution)/shard_map/all_to_all | solution.py:447
  136.0 0.0 copy-done.1
  136.0 0.0 copy-done
  136.0 2.7 %inverse.1 = (f32[16,4,2048]{2,1,0:T(4,128)}, f32[16,4,2048]{2,1,0:T(4,128)}, f32[16,4,2048]{2,1,0:T(4,128)}) custom-call(f32[2560,128]{1,0:T(8,128)S(1)} %bitcast.11, bf16[2,2,512,512]{3,2,1,0:T(8,128)(2,1)S(1)} %copy-done.1, bf16[2,2,512,512]{3,2,1,0:T(8,128)(2,1)S(1)} %copy-done), custom_call_target="tpu_custom_call" | custom-call | tf_op jit(solution)/shard_map/inverse/pallas_call | solution.py:430
Async XLA Ops:
  76.8 2.8 %copy-start.2 = (bf16[256,1024]{1,0:T(8,128)(2,1)S(1)}, bf16[256,1024]{1,0:T(8,128)(2,1)}, u32[]{:S(2)}) copy-start(bf16[256,1024]{1,0:T(8,128)(2,1)} %constant.43.clone.pl_ref) | copy-start | bytes 1572868
  76.8 2.9 %copy-start.3 = (bf16[256,1024]{1,0:T(8,128)(2,1)S(1)}, bf16[256,1024]{1,0:T(8,128)(2,1)}, u32[]{:S(2)}) copy-start(bf16[256,1024]{1,0:T(8,128)(2,1)} %constant.42.clone.ph_ref) | copy-start | bytes 1572868
  76.8 2.9 %copy-start.4 = (f32[2048]{0:T(1024)S(1)}, f32[2048]{0:T(1024)}, u32[]{:S(2)}) copy-start(f32[2048]{0:T(1024)} %constant.41.clone.gain_ref) | copy-start | bytes 24580
  76.8 2.9 %copy-start.5 = (f32[1,1024]{1,0:T(1,128)S(1)}, f32[1,1024]{1,0:T(1,128)}, u32[]{:S(2)}) copy-start(f32[1,1024]{1,0:T(1,128)} %constant.44.clone.wt_ref) | copy-start | bytes 12292
  76.8 2.9 %copy-start.6 = (f32[8]{0:T(128)S(1)}, f32[8]{0:T(128)}, u32[]{:S(2)}) copy-start(f32[8]{0:T(128)} %mu_ref.1) | copy-start | bytes 100
  76.8 2.9 %copy-start.7 = (f32[8]{0:T(128)S(1)}, f32[8]{0:T(128)}, u32[]{:S(2)}) copy-start(f32[8]{0:T(128)} %dec_ref.1) | copy-start | bytes 100
  76.8 2.9 %copy-start.8 = (f32[8]{0:T(128)S(1)}, f32[8]{0:T(128)}, u32[]{:S(2)}) copy-start(f32[8]{0:T(128)} %con_ref.1) | copy-start | bytes 100
  77.7 6.2 %collective-permute-start = (f32[1024,128]{1,0:T(8,128)}, f32[1024,128]{1,0:T(8,128)S(1)}, u32[]{:S(2)}, u32[]{:S(2)}) collective-permute-start(f32[1024,128]{1,0:T(8,128)} %half.1), channel_id=1, source_target_pairs={{0,8},{8,0},{1,9},{9,1},{2,10},{10,2},{3,11},{11,3},{4,12},{12,4},... | collective-permute-start | bytes 1572872 | tf_op jit(solution)/shard_map/ppermute | solution.py:464
  83.9 52.1 %copy-start.1 = (bf16[2,2,512,512]{3,2,1,0:T(8,128)(2,1)S(1)}, bf16[2,2,512,512]{3,2,1,0:T(8,128)(2,1)}, u32[]{:S(2)}) copy-start(bf16[2,2,512,512]{3,2,1,0:T(8,128)(2,1)} %constant.39.clone.th_hbm.th_ref) | copy-start | bytes 6291460
  87.8 48.2 %copy-start = (bf16[2,2,512,512]{3,2,1,0:T(8,128)(2,1)S(1)}, bf16[2,2,512,512]{3,2,1,0:T(8,128)(2,1)}, u32[]{:S(2)}) copy-start(bf16[2,2,512,512]{3,2,1,0:T(8,128)(2,1)} %constant.40.clone.tl_hbm.tl_ref) | copy-start | bytes 6291460
